TPU v7x, 256 devices: a whole 4x4x8 slice. The times are simulated.
256 devices in a mesh: seq: 32 (over y, z), batch: 8 (over x, core).
Axes of the slice: x: 4, y: 4, z: 8, core: 2. Of those that a mesh axis runs over, the one named last changes fastest.
Arguments:
- queries: bfloat16 [32768, 4096], P(('batch', 'seq')), parts along dimension 0
- keys: bfloat16 [32768, 4096], P(('batch', 'seq')), parts along dimension 0
- values: bfloat16 [32768, 4096], P(('batch', 'seq')), parts along dimension 0, may hold values from -6 to 6
- out_grad: bfloat16 [32768, 4096], P(('batch', 'seq')), parts along dimension 0, may hold values from -6 to 6
- key_blocks: int32 [256, 64, 12], P('batch'), parts along dimension 0, may hold values from -1 to 63, as said below
- dilation: int32 [256], P('batch'), parts along dimension 0, may hold values from 1 to 729, as said below
Outputs:
- attended: bfloat16 [32768, 4096], P(('batch', 'seq')), parts along dimension 0
- queries_grad: bfloat16 [32768, 4096], P(('batch', 'seq')), parts along dimension 0
- keys_grad: bfloat16 [32768, 4096], P(('batch', 'seq')), parts along dimension 0
- values_grad: bfloat16 [32768, 4096], P(('batch', 'seq')), parts along dimension 0
There are 8 independent parts, one for each index of `batch`. A program takes and returns all parts, laid end to end along the dimension named above; each array names one. Nothing has to cross between parts.
Inputs may be any that keep to these rules, and one draw needn't show every extreme that they name: `key_blocks`: in every row the first entry is the query block itself; the listed blocks are distinct, not after the query block, and stand before the -1 entries. Some head lists 12 blocks for each of its last query blocks. `dilation`: every value is a power of three.
All inputs are finite; a program needn't handle non-finite values.
Results may differ from a plain program's by a relative error of at most 0.012.
Values may be sent and summed in bfloat16 or wider, within the bound.
No kernel may reach another device: no remote copies, remote signals or barrier semaphores. Data moves between devices by JAX's collectives and lax.ppermute only.
A program may use at most 64 MiB of HBM per device.

v0:
```python
import math

import jax
import jax.numpy as jnp
from jax import lax
from jax.sharding import PartitionSpec as P

HEADS = 32
HEAD_DIM = 128
BLOCK = 64


very_low = -1e30


def tile_mask(group_ids, chosen, valid, spacing, block_size):
    offsets = lax.broadcasted_iota(jnp.int32, (block_size, block_size), 0) - lax.broadcasted_iota(
        jnp.int32, (block_size, block_size), 1
    )
    distance = ((group_ids[:, None] - chosen) * block_size)[:, None, :, None] + offsets[
        None, :, None, :
    ]
    allowed = valid[:, None, :, None] & (distance >= 0) & (distance % spacing == 0)
    return allowed.reshape(allowed.shape[0], block_size, chosen.shape[1] * block_size)


def group_scores(query_tile, key_rows, lists, group_ids, spacing, score_scale):
    group_size, block_size, head_size = query_tile.shape
    valid = lists >= 0
    chosen = jnp.maximum(lists, 0)
    keys_tile = key_rows[chosen].reshape(group_size, -1, head_size)
    allowed = tile_mask(group_ids, chosen, valid, spacing, block_size)
    raw_scores = (
        jnp.einsum("gae,gke->gak", query_tile, keys_tile, preferred_element_type=jnp.float32)
        * score_scale
    )
    return (chosen, keys_tile, jnp.where(allowed, raw_scores, very_low))


def grouped(array, group_size):
    return array.reshape((array.shape[0] // group_size, group_size) + array.shape[1:])


def head_forward(query_rows, key_rows, value_rows, block_rows, spacing, score_scale):
    number_rows, block_size, head_size = query_rows.shape
    group_size = min(512 // block_size, number_rows)
    all_ids = jnp.arange(number_rows, dtype=jnp.int32)

    def one_group(operands):
        query_tile, lists, group_ids = operands
        chosen, keys_tile, scores = group_scores(
            query_tile, key_rows, lists, group_ids, spacing, score_scale
        )
        row_top = jnp.max(scores, axis=2)
        expos = jnp.exp(scores - row_top[:, :, None])
        row_total = jnp.sum(expos, axis=2)
        weights = expos / row_total[:, :, None]
        values_tile = value_rows[chosen].reshape(query_tile.shape[0], -1, head_size)
        output_tile = jnp.einsum(
            "gak,gke->gae",
            weights.astype(jnp.bfloat16),
            values_tile,
            preferred_element_type=jnp.float32,
        ).astype(jnp.bfloat16)
        return (output_tile, row_top, row_total)

    outputs, tops, totals = lax.map(
        one_group,
        (
            grouped(query_rows, group_size),
            grouped(block_rows, group_size),
            grouped(all_ids, group_size),
        ),
    )
    return (
        outputs.reshape(query_rows.shape),
        tops.reshape(number_rows, block_size),
        totals.reshape(number_rows, block_size),
    )


def head_backward(
    query_rows,
    grad_rows,
    key_rows,
    value_rows,
    output_rows,
    tops,
    totals,
    block_rows,
    spacing,
    score_scale,
):
    number_rows, block_size, head_size = query_rows.shape
    group_size = min(512 // block_size, number_rows)
    all_ids = jnp.arange(number_rows, dtype=jnp.int32)

    def one_group(carried, operands):
        keys_sum, values_sum = carried
        query_tile, grad_tile, output_tile, row_top, row_total, lists, group_ids = operands
        chosen, keys_tile, scores = group_scores(
            query_tile, key_rows, lists, group_ids, spacing, score_scale
        )
        weights = jnp.exp(scores - row_top[:, :, None]) / row_total[:, :, None]
        weights16 = weights.astype(jnp.bfloat16)
        values_tile = value_rows[chosen].reshape(query_tile.shape[0], -1, head_size)
        delta = jnp.sum(grad_tile.astype(jnp.float32) * output_tile.astype(jnp.float32), axis=2)
        values_part = jnp.einsum(
            "gak,gae->gke", weights16, grad_tile, preferred_element_type=jnp.float32
        ).reshape(-1, block_size, head_size)
        dweights = jnp.einsum(
            "gae,gke->gak", grad_tile, values_tile, preferred_element_type=jnp.float32
        )
        dscores16 = (weights * (dweights - delta[:, :, None])).astype(jnp.bfloat16)
        query_part = (
            jnp.einsum("gak,gke->gae", dscores16, keys_tile, preferred_element_type=jnp.float32)
            * score_scale
        ).astype(jnp.bfloat16)
        keys_part = (
            jnp.einsum("gak,gae->gke", dscores16, query_tile, preferred_element_type=jnp.float32)
            * score_scale
        ).reshape(-1, block_size, head_size)
        flat_ids = chosen.reshape(-1)
        return (
            (keys_sum.at[flat_ids].add(keys_part), values_sum.at[flat_ids].add(values_part)),
            query_part,
        )

    zeros_start = jnp.zeros(key_rows.shape, jnp.float32)
    operands = (
        grouped(query_rows, group_size),
        grouped(grad_rows, group_size),
        grouped(output_rows, group_size),
        grouped(tops, group_size),
        grouped(totals, group_size),
        grouped(block_rows, group_size),
        grouped(all_ids, group_size),
    )
    (keys_sum, values_sum), query_parts = lax.scan(one_group, (zeros_start, zeros_start), operands)
    return (
        query_parts.reshape(query_rows.shape),
        keys_sum.astype(jnp.bfloat16),
        values_sum.astype(jnp.bfloat16),
    )


def head_lists(key_blocks, dilation, head_index):
    block_rows = lax.dynamic_index_in_dim(key_blocks, head_index, 0, keepdims=False)
    spacing = lax.dynamic_index_in_dim(dilation, head_index, 0, keepdims=False)
    return (block_rows, spacing)


def forward_all(
    blocked_queries,
    blocked_keys,
    blocked_values,
    key_blocks,
    dilation,
    my_index,
    local_heads,
    score_scale,
):
    outputs, stats = ([], [])
    block_rows, spacing = head_lists(key_blocks, dilation, my_index * local_heads + 0)
    output_rows, tops, totals = head_forward(
        blocked_queries, blocked_keys, blocked_values, block_rows, spacing, score_scale
    )
    outputs.append(output_rows)
    stats.append((tops, totals))
    return (outputs, stats)


def backward_all(
    blocked_queries,
    blocked_grads,
    blocked_keys,
    blocked_values,
    outputs,
    stats,
    key_blocks,
    dilation,
    my_index,
    local_heads,
    score_scale,
):
    collected = ([], [], [])
    block_rows, spacing = head_lists(key_blocks, dilation, my_index * local_heads + 0)
    results = head_backward(
        blocked_queries,
        blocked_grads,
        blocked_keys,
        blocked_values,
        outputs[0],
        stats[0][0],
        stats[0][1],
        block_rows,
        spacing,
        score_scale,
    )
    for bucket, result in zip(collected, results):
        bucket.append(result)
    return tuple((bucket[0] for bucket in collected))


def blocked_form(rows):
    return rows.reshape(rows.shape[0] // BLOCK, BLOCK, rows.shape[1])


def local(queries, keys, values, out_grad, key_blocks, dilation):
    devices = lax.axis_size("seq")
    my_index = lax.axis_index("seq")
    local_heads = HEADS // devices
    score_scale = 1.0 / math.sqrt(HEAD_DIM)
    heads_queries, heads_keys, heads_values, heads_grads = (
        lax.all_to_all(queries, "seq", split_axis=1, concat_axis=0, tiled=True),
        lax.all_to_all(keys, "seq", split_axis=1, concat_axis=0, tiled=True),
        lax.all_to_all(values, "seq", split_axis=1, concat_axis=0, tiled=True),
        lax.all_to_all(out_grad, "seq", split_axis=1, concat_axis=0, tiled=True),
    )
    seq_len, width_local = heads_queries.shape
    blocked_queries = blocked_form(heads_queries)
    blocked_keys = blocked_form(heads_keys)
    blocked_values = blocked_form(heads_values)
    outputs, stats = forward_all(
        blocked_queries,
        blocked_keys,
        blocked_values,
        key_blocks,
        dilation,
        my_index,
        local_heads,
        score_scale,
    )
    queries_grad, keys_grad, values_grad = backward_all(
        blocked_queries,
        blocked_form(heads_grads),
        blocked_keys,
        blocked_values,
        outputs,
        stats,
        key_blocks,
        dilation,
        my_index,
        local_heads,
        score_scale,
    )
    attended = outputs[0].reshape(seq_len, width_local)
    return (
        lax.all_to_all(attended, "seq", split_axis=0, concat_axis=1, tiled=True),
        lax.all_to_all(
            queries_grad.reshape(seq_len, width_local),
            "seq",
            split_axis=0,
            concat_axis=1,
            tiled=True,
        ),
        lax.all_to_all(
            keys_grad.reshape(seq_len, width_local), "seq", split_axis=0, concat_axis=1, tiled=True
        ),
        lax.all_to_all(
            values_grad.reshape(seq_len, width_local),
            "seq",
            split_axis=0,
            concat_axis=1,
            tiled=True,
        ),
    )


def solution(mesh):
    return jax.shard_map(
        local,
        mesh=mesh,
        in_specs=(
            P(("batch", "seq"), None),
            P(("batch", "seq"), None),
            P(("batch", "seq"), None),
            P(("batch", "seq"), None),
            P("batch", None, None),
            P("batch"),
        ),
        out_specs=(
            P(("batch", "seq"), None),
            P(("batch", "seq"), None),
            P(("batch", "seq"), None),
            P(("batch", "seq"), None),
        ),
        check_vma=False,
    )
```

profile of v0, /device:TPU:2, one launch (start us, length us, event | category | flops | bytes accessed | tf_op | source)
XLA Modules:
  0.0 1011.8 jit_solution(6852667675761783001)
XLA Ops:
  15.9 27.4 %all-to-all-done = bf16[128,32,128]{2,0,1:T(8,128)(2,1)S(1)} async-done(((bf16[128,32,128]{2,0,1:T(8,128)(2,1)}), bf16[128,32,128]{2,0,1:T(8,128)(2,1)S(1)}, u32[]{:S(2)}, u32[]{:S(2)}) %all-to-all-start) | async-done | bytes 1048608 | tf_op jit(solution)/shard_map/all_to_all | solution.py:215
  50.6 27.0 %all-to-all-done.1 = bf16[128,32,128]{2,0,1:T(8,128)(2,1)S(1)} async-done(((bf16[128,32,128]{2,0,1:T(8,128)(2,1)}), bf16[128,32,128]{2,0,1:T(8,128)(2,1)S(1)}, u32[]{:S(2)}, u32[]{:S(2)}) %all-to-all-start.1) | async-done | bytes 1048608 | tf_op jit(solution)/shard_map/all_to_all | solution.py:216
  87.9 23.0 %all-to-all-done.2 = bf16[128,32,128]{2,0,1:T(8,128)(2,1)S(1)} async-done(((bf16[128,32,128]{2,0,1:T(8,128)(2,1)}), bf16[128,32,128]{2,0,1:T(8,128)(2,1)S(1)}, u32[]{:S(2)}, u32[]{:S(2)}) %all-to-all-start.2) | async-done | bytes 1048608 | tf_op jit(solution)/shard_map/all_to_all | solution.py:217
  117.5 229.5 %while.32 = (s32[]{:T(128)}, bf16[8,8,64,128]{3,2,1,0:T(8,128)(2,1)}, f32[8,8,64]{2,1,0:T(8,128)S(1)}, f32[8,8,64]{2,1,0:T(8,128)S(1)}, s32[8,8,12]{2,1,0:T(8,12...) while((s32[]{:T(128)}, ...), condition=%wide.region_3.4_spmd, body=%wide.region_0.3_spmd.sunk | while | flops 209260928 | bytes 21687504 | solution.py:67
  122.0 17.6 %fusion.81 = (f32[8,64]{1,0:T(8,128)S(1)}, f32[8,64,768]{2,1,0:T(8,128)S(1)}) fusion(bf16[8,768,128]{2,1,0:T(8,128)(2,1)} %bitcast.182, bf16[8,8,64,128]{3,2,1,0:T(8,128)(2,1)} %get-tuple-element.578, s32[]{:T(128)S(6)} %copy.64, pred[]{:T(512)} %get-tuple-element.577, s32[]{:T(128)} %get-tuple-element.576, s32[64,768]{1,0:T(8,128)S(1)} %add.185, ...), kind=kOutput, calls=%fused_computation.86.clone.1 | convolution fusion | flops 106561024 | bytes 3507204 | tf_op jit(solution)/shard_map/while/body/eval_jaxpr/gae,gke->gak/dot_general | solution.py:34
  150.7 17.6 %fusion.81 = (f32[8,64]{1,0:T(8,128)S(1)}, f32[8,64,768]{2,1,0:T(8,128)S(1)}) fusion(bf16[8,768,128]{2,1,0:T(8,128)(2,1)} %bitcast.182, bf16[8,8,64,128]{3,2,1,0:T(8,128)(2,1)} %get-tuple-element.578, s32[]{:T(128)S(6)} %copy.64, pred[]{:T(512)} %get-tuple-element.577, s32[]{:T(128)} %get-tuple-element.576, s32[64,768]{1,0:T(8,128)S(1)} %add.185, ...), kind=kOutput, calls=%fused_computation.86.clone.1 | convolution fusion | flops 106561024 | bytes 3507204 | tf_op jit(solution)/shard_map/while/body/eval_jaxpr/gae,gke->gak/dot_general | solution.py:34
  179.4 17.6 %fusion.81 = (f32[8,64]{1,0:T(8,128)S(1)}, f32[8,64,768]{2,1,0:T(8,128)S(1)}) fusion(bf16[8,768,128]{2,1,0:T(8,128)(2,1)} %bitcast.182, bf16[8,8,64,128]{3,2,1,0:T(8,128)(2,1)} %get-tuple-element.578, s32[]{:T(128)S(6)} %copy.64, pred[]{:T(512)} %get-tuple-element.577, s32[]{:T(128)} %get-tuple-element.576, s32[64,768]{1,0:T(8,128)S(1)} %add.185, ...), kind=kOutput, calls=%fused_computation.86.clone.1 | convolution fusion | flops 106561024 | bytes 3507204 | tf_op jit(solution)/shard_map/while/body/eval_jaxpr/gae,gke->gak/dot_general | solution.py:34
  208.1 17.6 %fusion.81 = (f32[8,64]{1,0:T(8,128)S(1)}, f32[8,64,768]{2,1,0:T(8,128)S(1)}) fusion(bf16[8,768,128]{2,1,0:T(8,128)(2,1)} %bitcast.182, bf16[8,8,64,128]{3,2,1,0:T(8,128)(2,1)} %get-tuple-element.578, s32[]{:T(128)S(6)} %copy.64, pred[]{:T(512)} %get-tuple-element.577, s32[]{:T(128)} %get-tuple-element.576, s32[64,768]{1,0:T(8,128)S(1)} %add.185, ...), kind=kOutput, calls=%fused_computation.86.clone.1 | convolution fusion | flops 106561024 | bytes 3507204 | tf_op jit(solution)/shard_map/while/body/eval_jaxpr/gae,gke->gak/dot_general | solution.py:34
  236.7 17.6 %fusion.81 = (f32[8,64]{1,0:T(8,128)S(1)}, f32[8,64,768]{2,1,0:T(8,128)S(1)}) fusion(bf16[8,768,128]{2,1,0:T(8,128)(2,1)} %bitcast.182, bf16[8,8,64,128]{3,2,1,0:T(8,128)(2,1)} %get-tuple-element.578, s32[]{:T(128)S(6)} %copy.64, pred[]{:T(512)} %get-tuple-element.577, s32[]{:T(128)} %get-tuple-element.576, s32[64,768]{1,0:T(8,128)S(1)} %add.185, ...), kind=kOutput, calls=%fused_computation.86.clone.1 | convolution fusion | flops 106561024 | bytes 3507204 | tf_op jit(solution)/shard_map/while/body/eval_jaxpr/gae,gke->gak/dot_general | solution.py:34
  265.4 17.6 %fusion.81 = (f32[8,64]{1,0:T(8,128)S(1)}, f32[8,64,768]{2,1,0:T(8,128)S(1)}) fusion(bf16[8,768,128]{2,1,0:T(8,128)(2,1)} %bitcast.182, bf16[8,8,64,128]{3,2,1,0:T(8,128)(2,1)} %get-tuple-element.578, s32[]{:T(128)S(6)} %copy.64, pred[]{:T(512)} %get-tuple-element.577, s32[]{:T(128)} %get-tuple-element.576, s32[64,768]{1,0:T(8,128)S(1)} %add.185, ...), kind=kOutput, calls=%fused_computation.86.clone.1 | convolution fusion | flops 106561024 | bytes 3507204 | tf_op jit(solution)/shard_map/while/body/eval_jaxpr/gae,gke->gak/dot_general | solution.py:34
  294.1 17.6 %fusion.81 = (f32[8,64]{1,0:T(8,128)S(1)}, f32[8,64,768]{2,1,0:T(8,128)S(1)}) fusion(bf16[8,768,128]{2,1,0:T(8,128)(2,1)} %bitcast.182, bf16[8,8,64,128]{3,2,1,0:T(8,128)(2,1)} %get-tuple-element.578, s32[]{:T(128)S(6)} %copy.64, pred[]{:T(512)} %get-tuple-element.577, s32[]{:T(128)} %get-tuple-element.576, s32[64,768]{1,0:T(8,128)S(1)} %add.185, ...), kind=kOutput, calls=%fused_computation.86.clone.1 | convolution fusion | flops 106561024 | bytes 3507204 | tf_op jit(solution)/shard_map/while/body/eval_jaxpr/gae,gke->gak/dot_general | solution.py:34
  322.8 17.6 %fusion.81 = (f32[8,64]{1,0:T(8,128)S(1)}, f32[8,64,768]{2,1,0:T(8,128)S(1)}) fusion(bf16[8,768,128]{2,1,0:T(8,128)(2,1)} %bitcast.182, bf16[8,8,64,128]{3,2,1,0:T(8,128)(2,1)} %get-tuple-element.578, s32[]{:T(128)S(6)} %copy.64, pred[]{:T(512)} %get-tuple-element.577, s32[]{:T(128)} %get-tuple-element.576, s32[64,768]{1,0:T(8,128)S(1)} %add.185, ...), kind=kOutput, calls=%fused_computation.86.clone.1 | convolution fusion | flops 106561024 | bytes 3507204 | tf_op jit(solution)/shard_map/while/body/eval_jaxpr/gae,gke->gak/dot_general | solution.py:34
  361.5 535.2 %while.33 = (s32[]{:T(128)}, f32[64,64,128]{2,1,0:T(8,128)}, f32[64,64,128]{2,1,0:T(8,128)}, bf16[8,8,64,128]{3,2,1,0:T(8,128)(2,1)}, s32[8,8,12]{2,1,0:T(8,128)...) while((s32[]{:T(128)}, f32[64,64,128]{2,1,0:T(8,128)}, ...), condition=%wide.region_8.9_spmd, body=%wide.region_4.8_spmd.sunk | while | flops 513938304 | bytes 60868664 | solution.py:139
  383.3 17.6 %exponential_divide_fusion.2 = f32[8,64,768]{2,1,0:T(8,128)S(1)} fusion(bf16[8,768,128]{2,1,0:T(8,128)(2,1)} %bitcast.179, f32[8,64]{1,0:T(8,128)S(1)} %get-tuple-element.543, f32[8,64]{1,0:T(8,128)S(1)} %get-tuple-element.544, s32[]{:T(128)} %get-tuple-element.620, s32[64,768]{1,0:T(8,128)S(1)} %add.194, s32[8,768]{1,0:T(8,128)S(1)} %add.196, ...), kind=kOutput, calls=%fused_computation.45.clone.1 | convolution fusion | flops 106954752 | bytes 3509252 | tf_op jit(solution)/shard_map/while/body/eval_jaxpr/gae,gke->gak/dot_general | solution.py:34
  449.4 17.6 %exponential_divide_fusion.2 = f32[8,64,768]{2,1,0:T(8,128)S(1)} fusion(bf16[8,768,128]{2,1,0:T(8,128)(2,1)} %bitcast.179, f32[8,64]{1,0:T(8,128)S(1)} %get-tuple-element.543, f32[8,64]{1,0:T(8,128)S(1)} %get-tuple-element.544, s32[]{:T(128)} %get-tuple-element.620, s32[64,768]{1,0:T(8,128)S(1)} %add.194, s32[8,768]{1,0:T(8,128)S(1)} %add.196, ...), kind=kOutput, calls=%fused_computation.45.clone.1 | convolution fusion | flops 106954752 | bytes 3509252 | tf_op jit(solution)/shard_map/while/body/eval_jaxpr/gae,gke->gak/dot_general | solution.py:34
  514.4 17.6 %exponential_divide_fusion.2 = f32[8,64,768]{2,1,0:T(8,128)S(1)} fusion(bf16[8,768,128]{2,1,0:T(8,128)(2,1)} %bitcast.179, f32[8,64]{1,0:T(8,128)S(1)} %get-tuple-element.543, f32[8,64]{1,0:T(8,128)S(1)} %get-tuple-element.544, s32[]{:T(128)} %get-tuple-element.620, s32[64,768]{1,0:T(8,128)S(1)} %add.194, s32[8,768]{1,0:T(8,128)S(1)} %add.196, ...), kind=kOutput, calls=%fused_computation.45.clone.1 | convolution fusion | flops 106954752 | bytes 3509252 | tf_op jit(solution)/shard_map/while/body/eval_jaxpr/gae,gke->gak/dot_general | solution.py:34
  579.4 17.6 %exponential_divide_fusion.2 = f32[8,64,768]{2,1,0:T(8,128)S(1)} fusion(bf16[8,768,128]{2,1,0:T(8,128)(2,1)} %bitcast.179, f32[8,64]{1,0:T(8,128)S(1)} %get-tuple-element.543, f32[8,64]{1,0:T(8,128)S(1)} %get-tuple-element.544, s32[]{:T(128)} %get-tuple-element.620, s32[64,768]{1,0:T(8,128)S(1)} %add.194, s32[8,768]{1,0:T(8,128)S(1)} %add.196, ...), kind=kOutput, calls=%fused_computation.45.clone.1 | convolution fusion | flops 106954752 | bytes 3509252 | tf_op jit(solution)/shard_map/while/body/eval_jaxpr/gae,gke->gak/dot_general | solution.py:34
  644.3 17.6 %exponential_divide_fusion.2 = f32[8,64,768]{2,1,0:T(8,128)S(1)} fusion(bf16[8,768,128]{2,1,0:T(8,128)(2,1)} %bitcast.179, f32[8,64]{1,0:T(8,128)S(1)} %get-tuple-element.543, f32[8,64]{1,0:T(8,128)S(1)} %get-tuple-element.544, s32[]{:T(128)} %get-tuple-element.620, s32[64,768]{1,0:T(8,128)S(1)} %add.194, s32[8,768]{1,0:T(8,128)S(1)} %add.196, ...), kind=kOutput, calls=%fused_computation.45.clone.1 | convolution fusion | flops 106954752 | bytes 3509252 | tf_op jit(solution)/shard_map/while/body/eval_jaxpr/gae,gke->gak/dot_general | solution.py:34
  709.2 17.6 %exponential_divide_fusion.2 = f32[8,64,768]{2,1,0:T(8,128)S(1)} fusion(bf16[8,768,128]{2,1,0:T(8,128)(2,1)} %bitcast.179, f32[8,64]{1,0:T(8,128)S(1)} %get-tuple-element.543, f32[8,64]{1,0:T(8,128)S(1)} %get-tuple-element.544, s32[]{:T(128)} %get-tuple-element.620, s32[64,768]{1,0:T(8,128)S(1)} %add.194, s32[8,768]{1,0:T(8,128)S(1)} %add.196, ...), kind=kOutput, calls=%fused_computation.45.clone.1 | convolution fusion | flops 106954752 | bytes 3509252 | tf_op jit(solution)/shard_map/while/body/eval_jaxpr/gae,gke->gak/dot_general | solution.py:34
  774.3 17.6 %exponential_divide_fusion.2 = f32[8,64,768]{2,1,0:T(8,128)S(1)} fusion(bf16[8,768,128]{2,1,0:T(8,128)(2,1)} %bitcast.179, f32[8,64]{1,0:T(8,128)S(1)} %get-tuple-element.543, f32[8,64]{1,0:T(8,128)S(1)} %get-tuple-element.544, s32[]{:T(128)} %get-tuple-element.620, s32[64,768]{1,0:T(8,128)S(1)} %add.194, s32[8,768]{1,0:T(8,128)S(1)} %add.196, ...), kind=kOutput, calls=%fused_computation.45.clone.1 | convolution fusion | flops 106954752 | bytes 3509252 | tf_op jit(solution)/shard_map/while/body/eval_jaxpr/gae,gke->gak/dot_general | solution.py:34
  839.3 17.6 %exponential_divide_fusion.2 = f32[8,64,768]{2,1,0:T(8,128)S(1)} fusion(bf16[8,768,128]{2,1,0:T(8,128)(2,1)} %bitcast.179, f32[8,64]{1,0:T(8,128)S(1)} %get-tuple-element.543, f32[8,64]{1,0:T(8,128)S(1)} %get-tuple-element.544, s32[]{:T(128)} %get-tuple-element.620, s32[64,768]{1,0:T(8,128)S(1)} %add.194, s32[8,768]{1,0:T(8,128)S(1)} %add.196, ...), kind=kOutput, calls=%fused_computation.45.clone.1 | convolution fusion | flops 106954752 | bytes 3509252 | tf_op jit(solution)/shard_map/while/body/eval_jaxpr/gae,gke->gak/dot_general | solution.py:34
  896.7 24.3 %all-to-all-start.5 = ((bf16[32,128,128]{2,1,0:T(8,128)(2,1)}), bf16[32,128,128]{2,1,0:T(8,128)(2,1)}, u32[]{:S(2)}, u32[]{:S(2)}) async-start(bf16[32,128,128]{2,1,0:T(8,128)(2,1)} %bitcast.186), calls=%async_computation.5 | async-start | bytes 2097152 | tf_op jit(solution)/shard_map/all_to_all | solution.py:250
  922.1 25.9 %all-to-all-done.5 = bf16[32,128,128]{2,1,0:T(8,128)(2,1)} async-done(((bf16[32,128,128]{2,1,0:T(8,128)(2,1)}), bf16[32,128,128]{2,1,0:T(8,128)(2,1)}, u32[]{:S(2)}, u32[]{:S(2)}) %all-to-all-start.5) | async-done | bytes 1048608 | tf_op jit(solution)/shard_map/all_to_all | solution.py:250
  954.4 24.9 %all-to-all-done.6 = bf16[32,128,128]{2,1,0:T(8,128)(2,1)} async-done(((bf16[32,128,128]{2,1,0:T(8,128)(2,1)}), bf16[32,128,128]{2,1,0:T(8,128)(2,1)}, u32[]{:S(2)}, u32[]{:S(2)}) %all-to-all-start.6) | async-done | bytes 1048608 | tf_op jit(solution)/shard_map/all_to_all | solution.py:257
  (424 shorter events, 560.4 us)
Async XLA Ops:
  0.6 14.0 %copy-start.8 = (bf16[128,4096]{1,0:T(8,128)(2,1)S(1)}, bf16[128,4096]{1,0:T(8,128)(2,1)}, u32[]{:S(2)}) copy-start(bf16[128,4096]{1,0:T(8,128)(2,1)} %param.11) | copy-start | bytes 3145732
  3.1 40.1 %all-to-all-start = ((bf16[128,32,128]{2,0,1:T(8,128)(2,1)}), bf16[128,32,128]{2,0,1:T(8,128)(2,1)S(1)}, u32[]{:S(2)}, u32[]{:S(2)}) async-start(bf16[128,32,128]{2,0,1:T(8,128)(2,1)} %copy_bitcast_fusion.3), calls=%async_computation | async-start | bytes 2097152 | tf_op jit(solution)/shard_map/all_to_all | solution.py:215
  15.9 33.4 %copy-start.9 = (bf16[128,4096]{1,0:T(8,128)(2,1)S(1)}, bf16[128,4096]{1,0:T(8,128)(2,1)}, u32[]{:S(2)}) copy-start(bf16[128,4096]{1,0:T(8,128)(2,1)} %param.12) | copy-start | bytes 3145732
  44.2 33.4 %all-to-all-start.1 = ((bf16[128,32,128]{2,0,1:T(8,128)(2,1)}), bf16[128,32,128]{2,0,1:T(8,128)(2,1)S(1)}, u32[]{:S(2)}, u32[]{:S(2)}) async-start(bf16[128,32,128]{2,0,1:T(8,128)(2,1)} %copy_bitcast_fusion.2), calls=%async_computation.1 | async-start | bytes 2097152 | tf_op jit(solution)/shard_map/all_to_all | solution.py:216
  50.6 32.0 %copy-start.10 = (s32[32]{0:T(128)S(1)}, s32[32]{0:T(128)}, u32[]{:S(2)}) copy-start(s32[32]{0:T(128)} %param.15) | copy-start | bytes 388
  77.6 33.2 %all-to-all-start.2 = ((bf16[128,32,128]{2,0,1:T(8,128)(2,1)}), bf16[128,32,128]{2,0,1:T(8,128)(2,1)S(1)}, u32[]{:S(2)}, u32[]{:S(2)}) async-start(bf16[128,32,128]{2,0,1:T(8,128)(2,1)} %copy_bitcast_fusion.1), calls=%async_computation.2 | async-start | bytes 2097152 | tf_op jit(solution)/shard_map/all_to_all | solution.py:217
  110.8 236.2 %all-to-all-start.4 = ((bf16[128,32,128]{2,0,1:T(8,128)(2,1)}), bf16[128,32,128]{2,0,1:T(8,128)(2,1)}, u32[]{:S(2)}, u32[]{:S(2)}) async-start(bf16[128,32,128]{2,0,1:T(8,128)(2,1)} %copy_bitcast_fusion), calls=%async_computation.4 | async-start | bytes 2097152 | tf_op jit(solution)/shard_map/all_to_all | solution.py:218
  347.0 549.7 %all-to-all-start.3 = ((bf16[32,128,128]{2,1,0:T(8,128)(2,1)}), bf16[32,128,128]{2,1,0:T(8,128)(2,1)}, u32[]{:S(2)}, u32[]{:S(2)}) async-start(bf16[32,128,128]{2,1,0:T(8,128)(2,1)} %bitcast.183), calls=%async_computation.3 | async-start | bytes 2097152 | tf_op jit(solution)/shard_map/all_to_all | solution.py:249
  383.3 17.6 %copy-start.4 = (bf16[96,64,128]{2,1,0:T(8,128)(2,1)S(1)}, bf16[96,64,128]{2,1,0:T(8,128)(2,1)}, u32[]{:S(2)}) copy-start(bf16[96,64,128]{2,1,0:T(8,128)(2,1)} %gather_fusion.3) | copy-start | bytes 4718596 | tf_op jit(solution)/shard_map/while
  402.6 4.3 copy-start.3
  449.4 17.6 %copy-start.4 = (bf16[96,64,128]{2,1,0:T(8,128)(2,1)S(1)}, bf16[96,64,128]{2,1,0:T(8,128)(2,1)}, u32[]{:S(2)}) copy-start(bf16[96,64,128]{2,1,0:T(8,128)(2,1)} %gather_fusion.3) | copy-start | bytes 4718596 | tf_op jit(solution)/shard_map/while
  514.4 17.6 %copy-start.4 = (bf16[96,64,128]{2,1,0:T(8,128)(2,1)S(1)}, bf16[96,64,128]{2,1,0:T(8,128)(2,1)}, u32[]{:S(2)}) copy-start(bf16[96,64,128]{2,1,0:T(8,128)(2,1)} %gather_fusion.3) | copy-start | bytes 4718596 | tf_op jit(solution)/shard_map/while
  579.4 17.6 %copy-start.4 = (bf16[96,64,128]{2,1,0:T(8,128)(2,1)S(1)}, bf16[96,64,128]{2,1,0:T(8,128)(2,1)}, u32[]{:S(2)}) copy-start(bf16[96,64,128]{2,1,0:T(8,128)(2,1)} %gather_fusion.3) | copy-start | bytes 4718596 | tf_op jit(solution)/shard_map/while
  598.7 4.3 copy-start.3
  644.3 17.6 %copy-start.4 = (bf16[96,64,128]{2,1,0:T(8,128)(2,1)S(1)}, bf16[96,64,128]{2,1,0:T(8,128)(2,1)}, u32[]{:S(2)}) copy-start(bf16[96,64,128]{2,1,0:T(8,128)(2,1)} %gather_fusion.3) | copy-start | bytes 4718596 | tf_op jit(solution)/shard_map/while
  709.2 17.6 %copy-start.4 = (bf16[96,64,128]{2,1,0:T(8,128)(2,1)S(1)}, bf16[96,64,128]{2,1,0:T(8,128)(2,1)}, u32[]{:S(2)}) copy-start(bf16[96,64,128]{2,1,0:T(8,128)(2,1)} %gather_fusion.3) | copy-start | bytes 4718596 | tf_op jit(solution)/shard_map/while
  774.3 17.6 %copy-start.4 = (bf16[96,64,128]{2,1,0:T(8,128)(2,1)S(1)}, bf16[96,64,128]{2,1,0:T(8,128)(2,1)}, u32[]{:S(2)}) copy-start(bf16[96,64,128]{2,1,0:T(8,128)(2,1)} %gather_fusion.3) | copy-start | bytes 4718596 | tf_op jit(solution)/shard_map/while
  793.6 4.3 copy-start.3
  839.3 17.6 %copy-start.4 = (bf16[96,64,128]{2,1,0:T(8,128)(2,1)S(1)}, bf16[96,64,128]{2,1,0:T(8,128)(2,1)}, u32[]{:S(2)}) copy-start(bf16[96,64,128]{2,1,0:T(8,128)(2,1)} %gather_fusion.3) | copy-start | bytes 4718596 | tf_op jit(solution)/shard_map/while
  896.7 24.3 %copy-start.2 = (f32[64,64,128]{2,1,0:T(8,128)S(1)}, f32[64,64,128]{2,1,0:T(8,128)}, u32[]{:S(2)}) copy-start(f32[64,64,128]{2,1,0:T(8,128)} %get-tuple-element.300) | copy-start | bytes 6291460
  896.7 51.3 %all-to-all-start.5 = ((bf16[32,128,128]{2,1,0:T(8,128)(2,1)}), bf16[32,128,128]{2,1,0:T(8,128)(2,1)}, u32[]{:S(2)}, u32[]{:S(2)}) async-start(bf16[32,128,128]{2,1,0:T(8,128)(2,1)} %bitcast.186), calls=%async_computation.5 | async-start | bytes 2097152 | tf_op jit(solution)/shard_map/all_to_all | solution.py:250
  922.1 31.1 %copy-start.1 = (f32[64,64,128]{2,1,0:T(8,128)S(1)}, f32[64,64,128]{2,1,0:T(8,128)}, u32[]{:S(2)}) copy-start(f32[64,64,128]{2,1,0:T(8,128)} %get-tuple-element.301) | copy-start | bytes 6291460
  948.0 31.3 %all-to-all-start.6 = ((bf16[32,128,128]{2,1,0:T(8,128)(2,1)}), bf16[32,128,128]{2,1,0:T(8,128)(2,1)}, u32[]{:S(2)}, u32[]{:S(2)}) async-start(bf16[32,128,128]{2,1,0:T(8,128)(2,1)} %bitcast.185), calls=%async_computation.6 | async-start | bytes 2097152 | tf_op jit(solution)/shard_map/all_to_all | solution.py:257
  979.3 30.3 %all-to-all-start.7 = ((bf16[32,128,128]{2,1,0:T(8,128)(2,1)}), bf16[32,128,128]{2,1,0:T(8,128)(2,1)S(1)}, u32[]{:S(2)}, u32[]{:S(2)}) async-start(bf16[32,128,128]{2,1,0:T(8,128)(2,1)} %bitcast.184), calls=%async_computation.7 | async-start | bytes 2097152 | tf_op jit(solution)/shard_map/all_to_all | solution.py:260
  (23 other events, 46.5 us)
where the time goes:
time: 1030 us; the launch traced here: 1010 us
  matrix products  381 us (37%)
  other arithmetic  260 us (25%)
  waiting for transfers between devices  145 us (14%)
  local copies, waits for them, and re-layouts  137 us (13%)
  starting transfers between devices  71.4 us (7%)
  loops' own time  15.1 us (1%)
    dot_general x16, matrix products, group_scores(): jnp.einsum('gae,gke->gak', query_tile, keys_tile, preferred_element_type=...  282 us
    scatter-add x8, other arithmetic, one_group(): values_sum.at[flat_ids].add(values_part)  122 us
    scatter-add x8, other arithmetic, one_group(): keys_sum.at[flat_ids].add(keys_part)  121 us
    add x64, local copies, waits for them, and re-layouts, tile_mask(): ((group_ids[:, None] - chosen) * block_size)[:, None, :, None]  34.5 us
    gather x16, local copies, waits for them, and re-layouts, group_scores(): keys_tile = key_rows[chosen].reshape(group_size, -1, head_size)  31.7 us
    gather x16, local copies, waits for them, and re-layouts, one_group(): values_tile = value_rows[chosen].reshape(query_tile.shape[0], -1, head_size)  31.3 us
    dot_general x8, matrix products, one_group(): jnp.einsum('gak,gae->gke', dscores16, query_tile, preferred_element_type=...  27.4 us
    all_to_all x1, waiting for transfers between devices, local(): lax.all_to_all(queries, 'seq', split_axis=1, concat_axis=0, tiled=True)  27.4 us
  transfers between devices with their start and end apart: 8, of which 6 were waited for; matrix products, arithmetic and copies ran while one was open for 75% of the time, Pallas kernels for 0%

commit v1 on v0

v1 whole, which is shorter than its diff:
```python
import math

import jax
import jax.numpy as jnp
from jax import lax
from jax.experimental import pallas as pl
from jax.experimental.pallas import tpu as pltpu
from jax.sharding import PartitionSpec as P

HEADS = 32
HEAD_DIM = 128
BLOCK = 64
PAIR = 2 * BLOCK
SLOTS = 12
SCALE = 1.0 / math.sqrt(HEAD_DIM)
VERY_LOW = -1e30
PAIRS_PER_STEP = 2
VMEM_LIMIT = 40 << 20

f32 = jnp.float32
bf16 = jnp.bfloat16
NT = (((1,), (1,)), ((), ()))
NN = (((1,), (0,)), ((), ()))


def index_tables(lists, spacing):
    blocks = lists.shape[0]
    ids = jnp.arange(blocks, dtype=jnp.int32)[:, None]
    valid = lists >= 0
    load = jnp.maximum(lists, 0)
    store = jnp.where(valid, lists, blocks)
    residue = jnp.where(valid, jnp.mod((load - ids) * BLOCK, spacing), -1)
    residue = residue.reshape(blocks // 2, 2, SLOTS).transpose(0, 2, 1)
    residue = jnp.broadcast_to(residue[:, :, :, None], (blocks // 2, SLOTS, 2, BLOCK))
    residue = residue.reshape(blocks // 2, SLOTS, PAIR)
    residue = jnp.pad(residue, ((0, 0), (0, 16 - SLOTS), (0, 0)), constant_values=-1)
    key_at = lax.broadcasted_iota(jnp.int32, (BLOCK, PAIR), 0)
    query_at = lax.broadcasted_iota(jnp.int32, (BLOCK, PAIR), 1) % BLOCK
    offsets = jnp.mod(query_at - key_at, spacing)
    return load, store, residue, jnp.stack([jnp.where(query_at >= key_at, offsets, -2), offsets])


def side_by_side(rows):
    zero = jnp.zeros((BLOCK, HEAD_DIM), rows.dtype)
    return jnp.concatenate(
        [
            jnp.concatenate([rows[:BLOCK], zero], 1),
            jnp.concatenate([zero, rows[BLOCK:]], 1),
        ],
        0,
    )


def listed_pair(blocks_ref, load_ref, first):
    return jnp.concatenate(
        [
            jnp.concatenate(
                [blocks_ref[load_ref[first, s]], blocks_ref[load_ref[first + 1, s]]], 1
            )
            for s in range(SLOTS)
        ],
        0,
    )


def store_rows(out_ref, weights_t, blocks_ref, load_ref, pair, scale):
    weights = weights_t.T
    for half in range(2):
        rows = jnp.concatenate(
            [blocks_ref[load_ref[2 * pair + half, s]] for s in range(SLOTS)], 0
        )
        out = lax.dot_general(
            weights[half * BLOCK : (half + 1) * BLOCK], rows, NN, preferred_element_type=f32
        )
        if scale is not None:
            out = out * scale
        start = pl.multiple_of(pair * PAIR + half * BLOCK, BLOCK)
        out_ref[pl.ds(start, BLOCK), :] = out.astype(bf16)


def add_to_listed(sum_ref, parts, store_ref, first, group=4):
    for half in range(2):
        for start in range(0, SLOTS, group):
            slots = range(start, start + group)
            blocks = [store_ref[first + half, s] for s in slots]
            before = [sum_ref[b] for b in blocks]
            for s, b, old in zip(slots, blocks, before):
                sum_ref[b] = (
                    old
                    + parts[
                        s * BLOCK : (s + 1) * BLOCK, half * HEAD_DIM : (half + 1) * HEAD_DIM
                    ]
                )


def pair_forward(load_ref, residue_ref, offsets_ref, q_ref, k_ref, v_ref, weights_ref, o_ref, pair, slot):
    start = pl.multiple_of(pair * PAIR, PAIR)
    q_diag = side_by_side(q_ref[pl.ds(start, PAIR), :])
    keys = listed_pair(k_ref, load_ref, 2 * pair)
    scores = lax.dot_general(keys, q_diag, NT, preferred_element_type=f32)
    residue = residue_ref[pair]
    masked = [
        jnp.where(
            offsets_ref[0 if s == 0 else 1] == residue[s : s + 1],
            scores[s * BLOCK : (s + 1) * BLOCK],
            VERY_LOW,
        )
        for s in range(SLOTS)
    ]
    top = masked[0]
    for part in masked[1:]:
        top = jnp.maximum(top, part)
    top = jnp.max(top, axis=0, keepdims=True)
    expos = [jnp.exp2((part - top) * (SCALE * math.log2(math.e))) for part in masked]
    total = expos[0]
    for part in expos[1:]:
        total = total + part
    inverse = 1.0 / jnp.sum(total, axis=0, keepdims=True)
    weights_t = jnp.concatenate([(part * inverse).astype(bf16) for part in expos], 0)
    weights_ref[slot] = weights_t
    store_rows(o_ref, weights_t, v_ref, load_ref, pair, None)


def pair_backward(
    load_ref, store_ref, weights_ref, q_ref, k_ref, v_ref, g_ref, o_ref, dq_ref, k_sum, v_sum, pair, slot
):
    start = pl.multiple_of(pair * PAIR, PAIR)
    grads = g_ref[pl.ds(start, PAIR), :]
    outs = o_ref[pl.ds(start, PAIR), :]
    delta = jnp.sum((grads.astype(f32) * outs.astype(f32)).T, axis=0, keepdims=True)
    g_diag = side_by_side(grads)
    q_diag = side_by_side(q_ref[pl.ds(start, PAIR), :])
    values = listed_pair(v_ref, load_ref, 2 * pair)
    dweights = lax.dot_general(values, g_diag, NT, preferred_element_type=f32)
    weights_t = weights_ref[slot]
    dscores = (weights_t.astype(f32) * (dweights - delta)).astype(bf16)
    add_to_listed(
        v_sum,
        lax.dot_general(weights_t, g_diag, NN, preferred_element_type=f32),
        store_ref,
        2 * pair,
    )
    add_to_listed(
        k_sum,
        lax.dot_general(dscores, q_diag, NN, preferred_element_type=f32),
        store_ref,
        2 * pair,
    )
    store_rows(dq_ref, dscores, k_ref, load_ref, pair, SCALE)


SCALARS = pl.BlockSpec(memory_space=pltpu.SMEM)


def resident(shape):
    zeros = (0,) * len(shape)
    return pl.BlockSpec(shape, lambda step: zeros, pipeline_mode=pl.Buffered(1))


def head_forward(q, k, v, tables):
    load, _, residue, offsets = tables
    pairs = q.shape[0] // PAIR
    weights_shape = (pairs, SLOTS * BLOCK, PAIR)

    def body(load_ref, residue_ref, offsets_ref, q_ref, k_ref, v_ref, weights_ref, o_ref):
        for u in range(PAIRS_PER_STEP):
            pair = pl.program_id(0) * PAIRS_PER_STEP + u
            pair_forward(
                load_ref, residue_ref, offsets_ref, q_ref, k_ref, v_ref, weights_ref, o_ref, pair, u
            )

    return pl.pallas_call(
        body,
        grid=(pairs // PAIRS_PER_STEP,),
        in_specs=[SCALARS]
        + [resident(x.shape) for x in (residue, offsets, q, k, v)],
        out_specs=[
            pl.BlockSpec((PAIRS_PER_STEP,) + weights_shape[1:], lambda step: (step, 0, 0)),
            resident(q.shape),
        ],
        out_shape=[
            jax.ShapeDtypeStruct(weights_shape, bf16),
            jax.ShapeDtypeStruct(q.shape, bf16),
        ],
        cost_estimate=pl.CostEstimate(
            flops=20_000_000_000, transcendentals=3_000_000, bytes_accessed=10_000_000
        ),
        compiler_params=pltpu.CompilerParams(vmem_limit_bytes=VMEM_LIMIT),
        name="head_forward",
    )(load, residue, offsets, q, k, v)


def head_backward(q, k, v, g, o, weights, tables):
    load, store, _, _ = tables
    pairs = q.shape[0] // PAIR
    blocks = q.shape[0] // BLOCK

    def body(
        load_ref, store_ref, weights_ref, q_ref, k_ref, v_ref, g_ref, o_ref,
        dq_ref, dk_ref, dv_ref, k_sum, v_sum,
    ):
        @pl.when(pl.program_id(0) == 0)
        def _():
            k_sum[...] = jnp.zeros(k_sum.shape, f32)
            v_sum[...] = jnp.zeros(v_sum.shape, f32)

        for u in range(PAIRS_PER_STEP):
            pair = pl.program_id(0) * PAIRS_PER_STEP + u
            pair_backward(
                load_ref, store_ref, weights_ref, q_ref, k_ref, v_ref, g_ref, o_ref,
                dq_ref, k_sum, v_sum, pair, u,
            )

        @pl.when(pl.program_id(0) == pl.num_programs(0) - 1)
        def _():
            dk_ref[...] = (k_sum[:blocks] * SCALE).astype(bf16)
            dv_ref[...] = v_sum[:blocks].astype(bf16)

    return pl.pallas_call(
        body,
        grid=(pairs // PAIRS_PER_STEP,),
        in_specs=[
            SCALARS,
            SCALARS,
            pl.BlockSpec((PAIRS_PER_STEP, SLOTS * BLOCK, PAIR), lambda step: (step, 0, 0)),
        ]
        + [resident(x.shape) for x in (q, k, v, g, o)],
        out_specs=[resident(q.shape), resident(k.shape), resident(v.shape)],
        out_shape=[jax.ShapeDtypeStruct(x.shape, bf16) for x in (q, k, v)],
        scratch_shapes=[pltpu.VMEM((blocks + 1, BLOCK, HEAD_DIM), f32)] * 2,
        cost_estimate=pl.CostEstimate(
            flops=24_000_000_000, transcendentals=0, bytes_accessed=16_000_000
        ),
        compiler_params=pltpu.CompilerParams(vmem_limit_bytes=VMEM_LIMIT),
        name="head_backward",
    )(load, store, weights, q, k, v, g, o)


def to_heads(rows):
    return lax.all_to_all(rows, "seq", split_axis=1, concat_axis=0, tiled=True)


def to_tokens(head):
    devices = lax.axis_size("seq")
    by_device = head.reshape(devices, -1, HEAD_DIM)
    received = lax.all_to_all(by_device, "seq", split_axis=0, concat_axis=0, tiled=True)
    return received.transpose(1, 0, 2).reshape(by_device.shape[1], devices * HEAD_DIM)


def blocked(head):
    return head.reshape(-1, BLOCK, HEAD_DIM)


def local(queries, keys, values, out_grad, key_blocks, dilation):
    my_head = lax.axis_index("seq")
    tables = index_tables(
        lax.dynamic_index_in_dim(key_blocks, my_head, 0, keepdims=False),
        lax.dynamic_index_in_dim(dilation, my_head, 0, keepdims=False),
    )
    q = to_heads(queries)
    k = blocked(to_heads(keys))
    v = blocked(to_heads(values))
    g = to_heads(out_grad)
    weights, o = head_forward(q, k, v, tables)
    dq, dk, dv = head_backward(q, k, v, g, o, weights, tables)
    return to_tokens(o), to_tokens(dq), to_tokens(dk), to_tokens(dv)


def solution(mesh):
    rows = P(("batch", "seq"), None)
    return jax.shard_map(
        local,
        mesh=mesh,
        in_specs=(rows, rows, rows, rows, P("batch", None, None), P("batch")),
        out_specs=(rows, rows, rows, rows),
        check_vma=False,
    )
```

time: 1030 us -> 282 us (0.27); the launches traced: 1010 us -> 280 us
  matrix products: 381 us -> 0 us
  other arithmetic: 260 us -> 1.79 us
  local copies, waits for them, and re-layouts: 137 us -> 29.4 us
  blocking collectives: 0 us -> 66.8 us
  waiting for transfers between devices: 145 us -> 94.5 us
  Pallas kernels: 0 us -> 44.3 us
  starting transfers between devices: 71.4 us -> 41.5 us
  loops' own time: 15.1 us -> 0 us
    dot_general x56 -> x0, matrix products: 381 us -> none  [the longest x16 282 us: group_scores(): jnp.einsum('gae,gke->gak', query_tile, keys_tile, preferred_element_type=...]
    scatter-add x16 -> x0, other arithmetic: 244 us -> none  [the longest x8 122 us: one_group(): values_sum.at[flat_ids].add(values_part)]
    all_to_all x0 -> x2, blocking collectives: none -> 66.8 us  [to_tokens(): lax.all_to_all(by_device, 'seq', split_axis=0, concat_axis=0, tiled=True)]
    gather x32 -> x0, local copies, waits for them, and re-layouts: 62.9 us -> none  [the longest x16 31.7 us: group_scores(): keys_tile = key_rows[chosen].reshape(group_size, -1, head_size)]
    all_to_all x8 -> x6, waiting for transfers between devices: 145 us -> 94.5 us  [the longest x4 73.3 us: to_heads(): return lax.all_to_all(rows, 'seq', split_axis=1, concat_axis=0, tiled=True)]
    pallas_call x0 -> x2, Pallas kernels: none -> 44.3 us  [the longest x1 22.3 us: head_forward(): pl.pallas_call(body, grid=(pairs // PAIRS_PER_STEP,), in_specs=[SCALARS]...]
    add x64 -> x0, local copies, waits for them, and re-layouts: 34.5 us -> none  [tile_mask(): ((group_ids[:, None] - chosen) * block_size)[:, None, :, None]]
    all_to_all x8 -> x6, starting transfers between devices: 71.4 us -> 41.5 us  [the longest x4 26.6 us: to_heads(): return lax.all_to_all(rows, 'seq', split_axis=1, concat_axis=0, tiled=True)]
  transfers between devices with their start and end apart: 8 -> 6, of which waited for: 6 -> 5; matrix products, arithmetic and copies ran while one was open for 75% -> 7% of each run, Pallas kernels for 0% -> 16%
where the time goes in v1:
time: 282 us; the launch traced here: 280 us
  waiting for transfers between devices  94.5 us (34%)
  blocking collectives  66.8 us (24%)
  Pallas kernels  44.3 us (16%)
  starting transfers between devices  41.5 us (15%)
  local copies, waits for them, and re-layouts  29.4 us (10%)
    all_to_all x4, waiting for transfers between devices, to_heads(): return lax.all_to_all(rows, 'seq', split_axis=1, concat_axis=0, tiled=True)  73.3 us
    all_to_all x2, blocking collectives, to_tokens(): lax.all_to_all(by_device, 'seq', split_axis=0, concat_axis=0, tiled=True)  66.8 us
    all_to_all x4, starting transfers between devices, to_heads(): return lax.all_to_all(rows, 'seq', split_axis=1, concat_axis=0, tiled=True)  26.6 us
    pallas_call x1, Pallas kernels, head_forward(): pl.pallas_call(body, grid=(pairs // PAIRS_PER_STEP,), in_specs=[SCALARS]...  22.3 us
    pallas_call x1, Pallas kernels, head_backward(): pl.pallas_call(body, grid=(pairs // PAIRS_PER_STEP,), in_specs=[SCALARS,...  22 us
    all_to_all x2, waiting for transfers between devices, to_tokens(): lax.all_to_all(by_device, 'seq', split_axis=0, concat_axis=0, tiled=True)  21.2 us
    all_to_all x2, starting transfers between devices, to_tokens(): lax.all_to_all(by_device, 'seq', split_axis=0, concat_axis=0, tiled=True)  14.9 us
    unnamed x16, local copies, waits for them, and re-layouts  9.01 us
  transfers between devices with their start and end apart: 6, of which 5 were waited for; matrix products, arithmetic and copies ran while one was open for 7% of the time, Pallas kernels for 16%

profile of v1, /device:TPU:2, one launch (start us, length us, event | category | flops | bytes accessed | tf_op | source)
XLA Modules:
  0.0 280.3 jit_solution(16491924136463250823)
XLA Ops:
  1.9 1.3 copy_bitcast_fusion.7
  3.1 11.5 %all-to-all-start = ((bf16[128,32,128]{2,0,1:T(8,128)(2,1)}), bf16[128,32,128]{2,0,1:T(8,128)(2,1)S(1)}, u32[]{:S(2)}, u32[]{:S(2)}) async-start(bf16[128,32,128]{2,0,1:T(8,128)(2,1)} %copy_bitcast_fusion.7), calls=%async_computation | async-start | bytes 2097152 | tf_op jit(solution)/shard_map/all_to_all | solution.py:240
  14.6 2.5 copy_bitcast_fusion.6
  17.1 26.1 %all-to-all-done = bf16[128,32,128]{2,0,1:T(8,128)(2,1)S(1)} async-done(((bf16[128,32,128]{2,0,1:T(8,128)(2,1)}), bf16[128,32,128]{2,0,1:T(8,128)(2,1)S(1)}, u32[]{:S(2)}, u32[]{:S(2)}) %all-to-all-start) | async-done | bytes 1048608 | tf_op jit(solution)/shard_map/all_to_all | solution.py:240
  43.3 5.1 %all-to-all-start.1 = ((bf16[128,32,128]{2,0,1:T(8,128)(2,1)}), bf16[128,32,128]{2,0,1:T(8,128)(2,1)S(1)}, u32[]{:S(2)}, u32[]{:S(2)}) async-start(bf16[128,32,128]{2,0,1:T(8,128)(2,1)} %copy_bitcast_fusion.6), calls=%async_computation.1 | async-start | bytes 2097152 | tf_op jit(solution)/shard_map/all_to_all | solution.py:240
  48.3 2.5 copy_bitcast_fusion.5
  50.8 25.8 %all-to-all-done.1 = bf16[128,32,128]{2,0,1:T(8,128)(2,1)S(1)} async-done(((bf16[128,32,128]{2,0,1:T(8,128)(2,1)}), bf16[128,32,128]{2,0,1:T(8,128)(2,1)S(1)}, u32[]{:S(2)}, u32[]{:S(2)}) %all-to-all-start.1) | async-done | bytes 1048608 | tf_op jit(solution)/shard_map/all_to_all | solution.py:240
  76.6 5.0 %all-to-all-start.2 = ((bf16[128,32,128]{2,0,1:T(8,128)(2,1)}), bf16[128,32,128]{2,0,1:T(8,128)(2,1)}, u32[]{:S(2)}, u32[]{:S(2)}) async-start(bf16[128,32,128]{2,0,1:T(8,128)(2,1)} %copy_bitcast_fusion.5), calls=%async_computation.2 | async-start | bytes 2097152 | tf_op jit(solution)/shard_map/all_to_all | solution.py:240
  84.8 1.4 fusion.4
  86.2 2.5 copy_bitcast_fusion.4
  88.7 21.3 %all-to-all-done.2 = bf16[128,32,128]{2,0,1:T(8,128)(2,1)} async-done(((bf16[128,32,128]{2,0,1:T(8,128)(2,1)}), bf16[128,32,128]{2,0,1:T(8,128)(2,1)}, u32[]{:S(2)}, u32[]{:S(2)}) %all-to-all-start.2) | async-done | bytes 1048608 | tf_op jit(solution)/shard_map/all_to_all | solution.py:240
  110.0 5.0 %all-to-all-start.4 = ((bf16[128,32,128]{2,0,1:T(8,128)(2,1)}), bf16[128,32,128]{2,0,1:T(8,128)(2,1)}, u32[]{:S(2)}, u32[]{:S(2)}) async-start(bf16[128,32,128]{2,0,1:T(8,128)(2,1)} %copy_bitcast_fusion.4), calls=%async_computation.4 | async-start | bytes 2097152 | tf_op jit(solution)/shard_map/all_to_all | solution.py:240
  118.4 22.3 %head_forward.1 = (bf16[32,768,128]{2,1,0:T(8,128)(2,1)S(1)}, bf16[4096,128]{1,0:T(8,128)(2,1)S(1)}) custom-call(s32[64,12]{1,0:T(8,128)S(1)} %get-tuple-element.15.load_ref, s32[32,16,128]{2,1,0:T(8,128)S(1)} %pad.4.residue_ref, s32[2,64,128]{2,1,0:T(8,128)S(1)} %pad_add_fusion.offsets_ref, bf16[4096,128]{1,0:T(8,128)(2,1)S(1)} %bitcast.69, ...), custom_call_target="tpu_custom_call" | custom-call | flops 20000000000 | bytes 10000000 | tf_op jit(solution)/shard_map/head_forward/pallas_call | solution.py:172
  141.6 2.7 copy-done.6
  144.3 9.8 %all-to-all-start.3 = ((bf16[32,128,128]{2,1,0:T(8,128)(2,1)}), bf16[32,128,128]{2,1,0:T(8,128)(2,1)}, u32[]{:S(2)}, u32[]{:S(2)}) async-start(bf16[32,128,128]{2,1,0:T(8,128)(2,1)} %bitcast.74), calls=%async_computation.3 | async-start | bytes 2097152 | tf_op jit(solution)/shard_map/all_to_all | solution.py:246
  154.1 1.2 copy-done.3
  155.4 22.0 %head_backward.1 = (bf16[4096,128]{1,0:T(8,128)(2,1)S(1)}, bf16[64,64,128]{2,1,0:T(8,128)(2,1)S(1)}, bf16[64,64,128]{2,1,0:T(8,128)(2,1)S(1)}) custom-call(s32[64,12]{1,0:T(8,128)S(1)} %get-tuple-element.15.load_ref, s32[64,12]{1,0:T(8,128)S(1)} %get-tuple-element.14.store_ref, bf16[32,768,128]{2,1,0:T(8,128)(2,1)} %copy-done.6, ...), custom_call_target="tpu_custom_call" | custom-call | flops 24000000000 | bytes 16000000 | tf_op jit(solution)/shard_map/head_backward/pallas_call | solution.py:219
  180.3 1.5 all-to-all-done.3
  181.8 35.2 %all_to_all.90 = bf16[32,128,128]{2,1,0:T(8,128)(2,1)S(1)} all-to-all(bf16[32,128,128]{2,1,0:T(8,128)(2,1)} %bitcast.76), channel_id=1, replica_groups=mesh['seq'=32,'batch'=8] {'seq'}, dimensions={0} | all-to-all | bytes 2097152 | tf_op jit(solution)/shard_map/all_to_all | solution.py:246
  217.0 31.6 %all_to_all.91 = bf16[32,128,128]{2,1,0:T(8,128)(2,1)} all-to-all(bf16[32,128,128]{2,1,0:T(8,128)(2,1)} %bitcast.75), channel_id=1, replica_groups=mesh['seq'=32,'batch'=8] {'seq'}, dimensions={0} | all-to-all | bytes 2097152 | tf_op jit(solution)/shard_map/all_to_all | solution.py:246
  248.6 5.0 %all-to-all-start.7 = ((bf16[32,128,128]{2,1,0:T(8,128)(2,1)}), bf16[32,128,128]{2,1,0:T(8,128)(2,1)S(1)}, u32[]{:S(2)}, u32[]{:S(2)}) async-start(bf16[32,128,128]{2,1,0:T(8,128)(2,1)} %bitcast.73), calls=%async_computation.7 | async-start | bytes 2097152 | tf_op jit(solution)/shard_map/all_to_all | solution.py:246
  253.6 2.3 copy_bitcast_fusion.3
  257.1 2.3 copy_bitcast_fusion.2
  259.5 19.7 %all-to-all-done.7 = bf16[32,128,128]{2,1,0:T(8,128)(2,1)S(1)} async-done(((bf16[32,128,128]{2,1,0:T(8,128)(2,1)}), bf16[32,128,128]{2,1,0:T(8,128)(2,1)S(1)}, u32[]{:S(2)}, u32[]{:S(2)}) %all-to-all-start.7) | async-done | bytes 1048608 | tf_op jit(solution)/shard_map/all_to_all | solution.py:246
  (36 shorter events, 12.4 us)
Async XLA Ops:
  0.6 1.2 copy-start
  0.6 81.0 %copy-start.7 = (s32[32]{0:T(128)S(1)}, s32[32]{0:T(128)}, u32[]{:S(2)}) copy-start(s32[32]{0:T(128)} %param.11) | copy-start | bytes 388
  3.1 40.1 %all-to-all-start = ((bf16[128,32,128]{2,0,1:T(8,128)(2,1)}), bf16[128,32,128]{2,0,1:T(8,128)(2,1)S(1)}, u32[]{:S(2)}, u32[]{:S(2)}) async-start(bf16[128,32,128]{2,0,1:T(8,128)(2,1)} %copy_bitcast_fusion.7), calls=%async_computation | async-start | bytes 2097152 | tf_op jit(solution)/shard_map/all_to_all | solution.py:240
  43.3 33.4 %all-to-all-start.1 = ((bf16[128,32,128]{2,0,1:T(8,128)(2,1)}), bf16[128,32,128]{2,0,1:T(8,128)(2,1)S(1)}, u32[]{:S(2)}, u32[]{:S(2)}) async-start(bf16[128,32,128]{2,0,1:T(8,128)(2,1)} %copy_bitcast_fusion.6), calls=%async_computation.1 | async-start | bytes 2097152 | tf_op jit(solution)/shard_map/all_to_all | solution.py:240
  76.6 33.3 %all-to-all-start.2 = ((bf16[128,32,128]{2,0,1:T(8,128)(2,1)}), bf16[128,32,128]{2,0,1:T(8,128)(2,1)}, u32[]{:S(2)}, u32[]{:S(2)}) async-start(bf16[128,32,128]{2,0,1:T(8,128)(2,1)} %copy_bitcast_fusion.5), calls=%async_computation.2 | async-start | bytes 2097152 | tf_op jit(solution)/shard_map/all_to_all | solution.py:240
  110.0 34.3 %all-to-all-start.4 = ((bf16[128,32,128]{2,0,1:T(8,128)(2,1)}), bf16[128,32,128]{2,0,1:T(8,128)(2,1)}, u32[]{:S(2)}, u32[]{:S(2)}) async-start(bf16[128,32,128]{2,0,1:T(8,128)(2,1)} %copy_bitcast_fusion.4), calls=%async_computation.4 | async-start | bytes 2097152 | tf_op jit(solution)/shard_map/all_to_all | solution.py:240
  140.6 1.0 copy-start.2
  141.6 2.7 copy-start.6
  144.3 37.5 %all-to-all-start.3 = ((bf16[32,128,128]{2,1,0:T(8,128)(2,1)}), bf16[32,128,128]{2,1,0:T(8,128)(2,1)}, u32[]{:S(2)}, u32[]{:S(2)}) async-start(bf16[32,128,128]{2,1,0:T(8,128)(2,1)} %bitcast.74), calls=%async_computation.3 | async-start | bytes 2097152 | tf_op jit(solution)/shard_map/all_to_all | solution.py:246
  154.1 1.3 copy-start.3
  177.4 1.0 copy-start.1
  178.4 1.0 copy-start.4
  179.4 1.0 copy-start.5
  248.6 30.6 %all-to-all-start.7 = ((bf16[32,128,128]{2,1,0:T(8,128)(2,1)}), bf16[32,128,128]{2,1,0:T(8,128)(2,1)S(1)}, u32[]{:S(2)}, u32[]{:S(2)}) async-start(bf16[32,128,128]{2,1,0:T(8,128)(2,1)} %bitcast.73), calls=%async_computation.7 | async-start | bytes 2097152 | tf_op jit(solution)/shard_map/all_to_all | solution.py:246

commit v2 on v1

v2 whole, which is shorter than its diff:
```python
import math

import jax
import jax.numpy as jnp
from jax import lax
from jax.experimental import pallas as pl
from jax.experimental.pallas import tpu as pltpu
from jax.sharding import PartitionSpec as P

HEADS = 32
HEAD_DIM = 128
BLOCK = 64
PAIR = 2 * BLOCK
SLOTS = 12
SCALE = 1.0 / math.sqrt(HEAD_DIM)
VERY_LOW = -1e30
PAIRS_PER_STEP = 2
HEADS_PER_STEP = 16
VMEM_LIMIT = 40 << 20

f32 = jnp.float32
bf16 = jnp.bfloat16
NT = (((1,), (1,)), ((), ()))
NN = (((1,), (0,)), ((), ()))


def index_tables(lists, spacing):
    blocks = lists.shape[0]
    ids = jnp.arange(blocks, dtype=jnp.int32)[:, None]
    valid = lists >= 0
    listed_block = jnp.maximum(lists, 0)
    load = listed_block // 2 * 6 + listed_block % 2
    store = jnp.where(valid, lists, blocks)
    residue = jnp.where(valid, jnp.mod((listed_block - ids) * BLOCK, spacing), -1)
    residue = residue.reshape(blocks // 2, 2, SLOTS).transpose(0, 2, 1)
    residue = jnp.broadcast_to(residue[:, :, :, None], (blocks // 2, SLOTS, 2, BLOCK))
    residue = residue.reshape(blocks // 2, SLOTS, PAIR)
    residue = jnp.pad(residue, ((0, 0), (0, 16 - SLOTS), (0, 0)), constant_values=-1)
    key_at = lax.broadcasted_iota(jnp.int32, (BLOCK, PAIR), 0)
    query_at = lax.broadcasted_iota(jnp.int32, (BLOCK, PAIR), 1) % BLOCK
    offsets = jnp.mod(query_at - key_at, spacing)
    return load, store, residue, jnp.stack([jnp.where(query_at >= key_at, offsets, -2), offsets])


def side_by_side(rows):
    zero = jnp.zeros((BLOCK, HEAD_DIM), rows.dtype)
    return jnp.concatenate(
        [
            jnp.concatenate([rows[:BLOCK], zero], 1),
            jnp.concatenate([zero, rows[BLOCK:]], 1),
        ],
        0,
    )


def listed(packed_ref, load_ref, block, array):
    return [packed_ref[load_ref[block, s] + 2 * array] for s in range(SLOTS)]


def listed_pair(packed_ref, load_ref, first, array):
    left = listed(packed_ref, load_ref, first, array)
    right = listed(packed_ref, load_ref, first + 1, array)
    return jnp.concatenate(
        [jnp.concatenate([a, b], 1) for a, b in zip(left, right)], 0
    )


def pair_queries(packed_ref, pair):
    return packed_ref[pl.ds(6 * pair, 2)].reshape(PAIR, HEAD_DIM)


def rows_of_pair(weights_t, packed_ref, load_ref, pair, array):
    weights = weights_t.T
    outs = []
    for half in range(2):
        rows = jnp.concatenate(listed(packed_ref, load_ref, 2 * pair + half, array), 0)
        outs.append(
            lax.dot_general(
                weights[half * BLOCK : (half + 1) * BLOCK], rows, NN, preferred_element_type=f32
            )
        )
    return jnp.concatenate(outs, 0)


def add_to_listed(sum_ref, parts, store_ref, first, group=4):
    for half in range(2):
        for start in range(0, SLOTS, group):
            slots = range(start, start + group)
            blocks = [store_ref[first + half, s] for s in slots]
            before = [sum_ref[b] for b in blocks]
            for s, b, old in zip(slots, blocks, before):
                sum_ref[b] = (
                    old
                    + parts[
                        s * BLOCK : (s + 1) * BLOCK, half * HEAD_DIM : (half + 1) * HEAD_DIM
                    ]
                )


def pair_forward(load_ref, residue_ref, offsets_ref, qkv_ref, weights_ref, o_ref, pair, slot):
    q_diag = side_by_side(pair_queries(qkv_ref, pair))
    keys = listed_pair(qkv_ref, load_ref, 2 * pair, 1)
    scores = lax.dot_general(keys, q_diag, NT, preferred_element_type=f32)
    residue = residue_ref[pair]
    masked = [
        jnp.where(
            offsets_ref[0 if s == 0 else 1] == residue[s : s + 1],
            scores[s * BLOCK : (s + 1) * BLOCK],
            VERY_LOW,
        )
        for s in range(SLOTS)
    ]
    top = masked[0]
    for part in masked[1:]:
        top = jnp.maximum(top, part)
    top = jnp.max(top, axis=0, keepdims=True)
    expos = [jnp.exp2((part - top) * (SCALE * math.log2(math.e))) for part in masked]
    total = expos[0]
    for part in expos[1:]:
        total = total + part
    inverse = 1.0 / jnp.sum(total, axis=0, keepdims=True)
    weights_t = jnp.concatenate([(part * inverse).astype(bf16) for part in expos], 0)
    weights_ref[slot] = weights_t
    o_ref[pair] = rows_of_pair(weights_t, qkv_ref, load_ref, pair, 2).astype(bf16)


def pair_backward(
    load_ref, store_ref, weights_ref, qkv_ref, g_ref, o_ref, grads_ref, k_sum, v_sum, pair, slot
):
    grads = g_ref[pair]
    delta = jnp.sum((grads.astype(f32) * o_ref[pair].astype(f32)).T, axis=0, keepdims=True)
    g_diag = side_by_side(grads)
    q_diag = side_by_side(pair_queries(qkv_ref, pair))
    values = listed_pair(qkv_ref, load_ref, 2 * pair, 2)
    dweights = lax.dot_general(values, g_diag, NT, preferred_element_type=f32)
    weights_t = weights_ref[slot]
    dscores = (weights_t.astype(f32) * (dweights - delta)).astype(bf16)
    add_to_listed(
        v_sum,
        lax.dot_general(weights_t, g_diag, NN, preferred_element_type=f32),
        store_ref,
        2 * pair,
    )
    add_to_listed(
        k_sum,
        lax.dot_general(dscores, q_diag, NN, preferred_element_type=f32),
        store_ref,
        2 * pair,
    )
    grads_ref[pair, 0] = (rows_of_pair(dscores, qkv_ref, load_ref, pair, 1) * SCALE).astype(bf16)


SCALARS = pl.BlockSpec(memory_space=pltpu.SMEM)


def resident(shape):
    zeros = (0,) * len(shape)
    return pl.BlockSpec(shape, lambda step: zeros, pipeline_mode=pl.Buffered(1))


def head_forward(qkv, tables):
    load, _, residue, offsets = tables
    pairs = residue.shape[0]
    weights_shape = (pairs, SLOTS * BLOCK, PAIR)
    out_shape = (pairs, PAIR, HEAD_DIM)

    def body(load_ref, residue_ref, offsets_ref, qkv_ref, weights_ref, o_ref):
        for u in range(PAIRS_PER_STEP):
            pair = pl.program_id(0) * PAIRS_PER_STEP + u
            pair_forward(
                load_ref, residue_ref, offsets_ref, qkv_ref, weights_ref, o_ref, pair, u
            )

    return pl.pallas_call(
        body,
        grid=(pairs // PAIRS_PER_STEP,),
        in_specs=[SCALARS] + [resident(x.shape) for x in (residue, offsets, qkv)],
        out_specs=[
            pl.BlockSpec((PAIRS_PER_STEP,) + weights_shape[1:], lambda step: (step, 0, 0)),
            resident(out_shape),
        ],
        out_shape=[
            pltpu.HBM(weights_shape, bf16),
            jax.ShapeDtypeStruct(out_shape, bf16),
        ],
        cost_estimate=pl.CostEstimate(
            flops=20_000_000_000, transcendentals=3_000_000, bytes_accessed=10_000_000
        ),
        compiler_params=pltpu.CompilerParams(vmem_limit_bytes=VMEM_LIMIT),
        name="head_forward",
    )(load, residue, offsets, qkv)


def head_backward(qkv, g, o, weights, tables):
    load, store, _, _ = tables
    pairs = g.shape[0]
    blocks = 2 * pairs
    grads_shape = (pairs, 3, PAIR, HEAD_DIM)

    def body(
        load_ref, store_ref, weights_ref, qkv_ref, g_ref, o_ref, grads_ref, k_sum, v_sum
    ):
        @pl.when(pl.program_id(0) == 0)
        def _():
            k_sum[...] = jnp.zeros(k_sum.shape, f32)
            v_sum[...] = jnp.zeros(v_sum.shape, f32)

        for u in range(PAIRS_PER_STEP):
            pair = pl.program_id(0) * PAIRS_PER_STEP + u
            pair_backward(
                load_ref, store_ref, weights_ref, qkv_ref, g_ref, o_ref, grads_ref,
                k_sum, v_sum, pair, u,
            )

        @pl.when(pl.program_id(0) == pl.num_programs(0) - 1)
        def _():
            by_pair = (pairs, PAIR, HEAD_DIM)
            grads_ref[:, 1] = (k_sum[:blocks] * SCALE).astype(bf16).reshape(by_pair)
            grads_ref[:, 2] = v_sum[:blocks].astype(bf16).reshape(by_pair)

    return pl.pallas_call(
        body,
        grid=(pairs // PAIRS_PER_STEP,),
        in_specs=[
            SCALARS,
            SCALARS,
            pl.BlockSpec((PAIRS_PER_STEP, SLOTS * BLOCK, PAIR), lambda step: (step, 0, 0)),
        ]
        + [resident(x.shape) for x in (qkv, g, o)],
        out_specs=resident(grads_shape),
        out_shape=jax.ShapeDtypeStruct(grads_shape, bf16),
        scratch_shapes=[pltpu.VMEM((blocks + 1, BLOCK, HEAD_DIM), f32)] * 2,
        cost_estimate=pl.CostEstimate(
            flops=24_000_000_000, transcendentals=0, bytes_accessed=16_000_000
        ),
        compiler_params=pltpu.CompilerParams(vmem_limit_bytes=VMEM_LIMIT),
        name="head_backward",
    )(load, store, weights, qkv, g, o)


def exchange(by_device):
    return lax.all_to_all(by_device, "seq", split_axis=0, concat_axis=0, tiled=True)


def in_hbm(array):
    return pltpu.with_memory_space_constraint(array, pltpu.HBM)


def pack_heads(*arrays):
    tokens, width = arrays[0].shape
    number = len(arrays)

    def body(*refs):
        for a in range(number):
            for h in range(HEADS_PER_STEP):
                refs[number][h, a] = refs[a][:, h * HEAD_DIM : (h + 1) * HEAD_DIM]

    return pl.pallas_call(
        body,
        grid=(width // HEAD_DIM // HEADS_PER_STEP,),
        in_specs=[pl.BlockSpec((tokens, HEADS_PER_STEP * HEAD_DIM), lambda step: (0, step))]
        * number,
        out_specs=pl.BlockSpec(
            (HEADS_PER_STEP, number, tokens, HEAD_DIM), lambda step: (step, 0, 0, 0)
        ),
        out_shape=pltpu.HBM((width // HEAD_DIM, number, tokens, HEAD_DIM), bf16),
        compiler_params=pltpu.CompilerParams(vmem_limit_bytes=24 << 20),
        name="pack_heads",
    )(*[in_hbm(x) for x in arrays])


def unpack_heads(packed):
    heads, number, tokens, _ = packed.shape

    def body(packed_ref, *out_refs):
        for a in range(number):
            for h in range(HEADS_PER_STEP):
                out_refs[a][:, h * HEAD_DIM : (h + 1) * HEAD_DIM] = packed_ref[h, a]

    return pl.pallas_call(
        body,
        grid=(heads // HEADS_PER_STEP,),
        in_specs=[
            pl.BlockSpec((HEADS_PER_STEP, number, tokens, HEAD_DIM), lambda step: (step, 0, 0, 0))
        ],
        out_specs=[pl.BlockSpec((tokens, HEADS_PER_STEP * HEAD_DIM), lambda step: (0, step))]
        * number,
        out_shape=[jax.ShapeDtypeStruct((tokens, heads * HEAD_DIM), bf16)] * number,
        compiler_params=pltpu.CompilerParams(vmem_limit_bytes=24 << 20),
        name="unpack_heads",
    )(packed)


def local(queries, keys, values, out_grad, key_blocks, dilation):
    my_head = lax.axis_index("seq")
    tables = index_tables(
        lax.dynamic_index_in_dim(key_blocks, my_head, 0, keepdims=False),
        lax.dynamic_index_in_dim(dilation, my_head, 0, keepdims=False),
    )
    qkv = exchange(pack_heads(queries, keys, values)).reshape(-1, BLOCK, HEAD_DIM)
    g = exchange(pack_heads(out_grad)).reshape(-1, PAIR, HEAD_DIM)
    weights, o = head_forward(qkv, tables)
    attended = exchange(o[:, None])
    grads = exchange(head_backward(qkv, g, o, weights, tables))
    return tuple(unpack_heads(attended)) + tuple(unpack_heads(grads))


def solution(mesh):
    rows = P(("batch", "seq"), None)
    return jax.shard_map(
        local,
        mesh=mesh,
        in_specs=(rows, rows, rows, rows, P("batch", None, None), P("batch")),
        out_specs=(rows, rows, rows, rows),
        check_vma=False,
    )
```

time: 282 us -> 249 us (0.88)
  blocking collectives: 66.8 us -> 0 us
  waiting for transfers between devices: 94.5 us -> 142 us
  local copies, waits for them, and re-layouts: 29.4 us -> 15 us
  Pallas kernels: 44.3 us -> 52.8 us
  starting transfers between devices: 41.5 us -> 35.1 us
    all_to_all x2 -> x0, blocking collectives: 66.8 us -> none  [to_tokens(): lax.all_to_all(by_device, 'seq', split_axis=0, concat_axis=0, tiled=True)]
    all_to_all x6 -> x4, waiting for transfers between devices: 94.5 us -> 142 us  [exchange(): lax.all_to_all(by_device, 'seq', split_axis=0, concat_axis=0, tiled=True)]
    all_to_all x4 -> x0, local copies, waits for them, and re-layouts: 8.73 us -> none  [to_heads(): return lax.all_to_all(rows, 'seq', split_axis=1, concat_axis=0, tiled=True)]
    pallas_call x0 -> x4, Pallas kernels: none -> 8.6 us  [the longest x2 5.43 us: pack_heads(): pl.pallas_call(body, grid=(width // HEAD_DIM // HEADS_PER_STEP,), in_spec...]
    reshape x4 -> x0, local copies, waits for them, and re-layouts: 6.94 us -> none  [to_tokens(): received.transpose(1, 0, 2).reshape(by_device.shape[1], devices * HEAD_DIM)]
    all_to_all x6 -> x4, starting transfers between devices: 41.5 us -> 35.1 us  [exchange(): lax.all_to_all(by_device, 'seq', split_axis=0, concat_axis=0, tiled=True)]
    unnamed x16 -> x18, local copies, waits for them, and re-layouts: 9.01 us -> 7.93 us
  transfers between devices with their start and end apart: 6 -> 4, of which waited for: 5 -> 3; matrix products, arithmetic and copies ran while one was open for 7% -> 4% of each run, Pallas kernels for 16% -> 19%
where the time goes in v2:
time: 249 us
  waiting for transfers between devices  142 us (57%)
  Pallas kernels  52.8 us (21%)
  starting transfers between devices  35.1 us (14%)
  local copies, waits for them, and re-layouts  15 us (6%)
    all_to_all x4, waiting for transfers between devices, exchange(): lax.all_to_all(by_device, 'seq', split_axis=0, concat_axis=0, tiled=True)  142 us
    all_to_all x4, starting transfers between devices, exchange(): lax.all_to_all(by_device, 'seq', split_axis=0, concat_axis=0, tiled=True)  35.1 us
    pallas_call x1, Pallas kernels, head_forward(): pl.pallas_call(body, grid=(pairs // PAIRS_PER_STEP,), in_specs=[SCALARS]...  22.8 us
    pallas_call x1, Pallas kernels, head_backward(): pl.pallas_call(body, grid=(pairs // PAIRS_PER_STEP,), in_specs=[SCALARS,...  21.4 us
    unnamed x18, local copies, waits for them, and re-layouts  7.93 us
    pallas_call x2, Pallas kernels, pack_heads(): pl.pallas_call(body, grid=(width // HEAD_DIM // HEADS_PER_STEP,), in_spec...  5.43 us
  transfers between devices with their start and end apart: 4, of which 3 were waited for; matrix products, arithmetic and copies ran while one was open for 4% of the time, Pallas kernels for 19%

profile of v2, /device:TPU:2, one launch (start us, length us, event | category | flops | bytes accessed | tf_op | source)
XLA Modules:
  0.0 248.8 jit_solution(13453190450469589444)
XLA Ops:
  0.6 3.3 %pack_heads.2 = bf16[32,3,128,128]{3,2,1,0:T(8,128)(2,1)} custom-call(bf16[128,4096]{1,0:T(8,128)(2,1)} %refs_0_.2, bf16[128,4096]{1,0:T(8,128)(2,1)} %refs_1_.1, bf16[128,4096]{1,0:T(8,128)(2,1)} %refs_2_.1), custom_call_target="tpu_custom_call" | custom-call | tf_op jit(solution)/shard_map/pack_heads/pallas_call | solution.py:258
  4.0 11.6 %all-to-all-start = ((bf16[32,3,128,128]{3,2,1,0:T(8,128)(2,1)}), bf16[32,3,128,128]{3,2,1,0:T(8,128)(2,1)S(1)}, u32[]{:S(2)}, u32[]{:S(2)}) async-start(bf16[32,3,128,128]{3,2,1,0:T(8,128)(2,1)} %pack_heads.2), calls=%async_computation | async-start | bytes 6291456 | tf_op jit(solution)/shard_map/all_to_all | solution.py:242
  17.9 2.1 pack_heads.3
  20.1 1.4 fusion.6
  21.4 68.8 %all-to-all-done = bf16[32,3,128,128]{3,2,1,0:T(8,128)(2,1)S(1)} async-done(((bf16[32,3,128,128]{3,2,1,0:T(8,128)(2,1)}), bf16[32,3,128,128]{3,2,1,0:T(8,128)(2,1)S(1)}, u32[]{:S(2)}, u32[]{:S(2)}) %all-to-all-start) | async-done | bytes 3145760 | tf_op jit(solution)/shard_map/all_to_all | solution.py:242
  90.3 5.9 %all-to-all-start.2 = ((bf16[32,1,128,128]{3,2,1,0:T(8,128)(2,1)}), bf16[32,1,128,128]{3,2,1,0:T(8,128)(2,1)}, u32[]{:S(2)}, u32[]{:S(2)}) async-start(bf16[32,1,128,128]{3,2,1,0:T(8,128)(2,1)} %pack_heads.3), calls=%async_computation.2 | async-start | bytes 2097152 | tf_op jit(solution)/shard_map/all_to_all | solution.py:242
  96.6 1.0 copy.28
  97.6 2.1 broadcast_in_dim.20
  99.7 1.9 reshape.204
  101.6 1.0 copy.29
  102.7 22.8 %head_forward.1 = (bf16[32,768,128]{2,1,0:T(8,128)(2,1)}, bf16[32,128,128]{2,1,0:T(8,128)(2,1)S(1)}) custom-call(s32[64,12]{1,0:T(8,128)S(1)} %get-tuple-element.15.load_ref, s32[32,16,128]{2,1,0:T(8,128)S(1)} %pad.4.residue_ref, s32[2,64,128]{2,1,0:T(8,128)S(1)} %pad_add_fusion.offsets_ref, bf16[192,64,128]{2,1,0:T(8,128)(2,1)S(1)} %bitcast.14), custom_call_target="tpu_custom_call" | custom-call | flops 20000000000 | bytes 10000000 | tf_op jit(solution)/shard_map/head_forward/pallas_call | solution.py:174
  125.5 1.0 copy-done.6
  126.5 9.7 %all-to-all-start.1 = ((bf16[32,1,128,128]{3,2,1,0:T(8,128)(2,1)}), bf16[32,1,128,128]{3,2,1,0:T(8,128)(2,1)S(1)}, u32[]{:S(2)}, u32[]{:S(2)}) async-start(bf16[32,1,128,128]{3,2,1,0:T(8,128)(2,1)} %bitcast.16), calls=%async_computation.1 | async-start | bytes 2097152 | tf_op jit(solution)/shard_map/all_to_all | solution.py:242
  136.2 1.9 copy-done.4
  138.1 1.2 copy-done.7
  139.3 21.4 %head_backward.1 = bf16[32,3,128,128]{3,2,1,0:T(8,128)(2,1)S(1)} custom-call(s32[64,12]{1,0:T(8,128)S(1)} %get-tuple-element.15.load_ref, s32[64,12]{1,0:T(8,128)S(1)} %get-tuple-element.14.store_ref, bf16[32,768,128]{2,1,0:T(8,128)(2,1)} %get-tuple-element.10.weights_ref, bf16[192,64,128]{2,1,0:T(8,128)(2,1)S(1)} %bitcast.15, ...), custom_call_target="tpu_custom_call" | custom-call | flops 24000000000 | bytes 16000000 | tf_op jit(solution)/shard_map/head_backward/pallas_call | solution.py:221
  160.7 1.6 copy-done.5
  162.4 1.9 all-to-all-done.1.packed_ref
  164.3 1.0 copy-done.1
  165.3 7.8 %all-to-all-start.3 = ((bf16[32,3,128,128]{3,2,1,0:T(8,128)(2,1)}), bf16[32,3,128,128]{3,2,1,0:T(8,128)(2,1)S(1)}, u32[]{:S(2)}, u32[]{:S(2)}) async-start(bf16[32,3,128,128]{3,2,1,0:T(8,128)(2,1)} %copy-done.5), calls=%async_computation.3 | async-start | bytes 6291456 | tf_op jit(solution)/shard_map/all_to_all | solution.py:242
  173.2 1.2 copy-done.2
  174.4 1.1 unpack_heads.2
  175.5 71.2 %all-to-all-done.3.packed_ref = bf16[32,3,128,128]{3,2,1,0:T(8,128)(2,1)S(1)} async-done(((bf16[32,3,128,128]{3,2,1,0:T(8,128)(2,1)}), bf16[32,3,128,128]{3,2,1,0:T(8,128)(2,1)S(1)}, u32[]{:S(2)}, u32[]{:S(2)}) %all-to-all-start.3) | async-done | bytes 3145760 | tf_op jit(solution)/shard_map/all_to_all | solution.py:242
  246.7 2.1 unpack_heads.3
  (28 shorter events, 1.4 us)
Async XLA Ops:
  0.6 16.9 %copy-start = (s32[32,64,12]{1,0,2:T(8,128)S(1)}, s32[32,64,12]{1,0,2:T(8,128)}, u32[]{:S(2)}) copy-start(s32[32,64,12]{1,0,2:T(8,128)} %param.10) | copy-start | bytes 294916
  4.0 11.6 %copy-start.8 = (s32[32]{0:T(128)S(1)}, s32[32]{0:T(128)}, u32[]{:S(2)}) copy-start(s32[32]{0:T(128)} %param.11) | copy-start | bytes 388
  4.0 86.3 %all-to-all-start = ((bf16[32,3,128,128]{3,2,1,0:T(8,128)(2,1)}), bf16[32,3,128,128]{3,2,1,0:T(8,128)(2,1)S(1)}, u32[]{:S(2)}, u32[]{:S(2)}) async-start(bf16[32,3,128,128]{3,2,1,0:T(8,128)(2,1)} %pack_heads.2), calls=%async_computation | async-start | bytes 6291456 | tf_op jit(solution)/shard_map/all_to_all | solution.py:242
  90.3 35.2 %copy-start.3 = (bf16[32,3,128,128]{3,2,1,0:T(8,128)(2,1)}, bf16[32,3,128,128]{3,2,1,0:T(8,128)(2,1)S(1)}, u32[]{:S(2)}) copy-start(bf16[32,3,128,128]{3,2,1,0:T(8,128)(2,1)S(1)} %all-to-all-done) | copy-start | bytes 9437188
  90.3 36.2 %all-to-all-start.2 = ((bf16[32,1,128,128]{3,2,1,0:T(8,128)(2,1)}), bf16[32,1,128,128]{3,2,1,0:T(8,128)(2,1)}, u32[]{:S(2)}, u32[]{:S(2)}) async-start(bf16[32,1,128,128]{3,2,1,0:T(8,128)(2,1)} %pack_heads.3), calls=%async_computation.2 | async-start | bytes 2097152 | tf_op jit(solution)/shard_map/all_to_all | solution.py:242
  125.5 1.0 copy-start.6
  126.5 37.9 %all-to-all-start.1 = ((bf16[32,1,128,128]{3,2,1,0:T(8,128)(2,1)}), bf16[32,1,128,128]{3,2,1,0:T(8,128)(2,1)S(1)}, u32[]{:S(2)}, u32[]{:S(2)}) async-start(bf16[32,1,128,128]{3,2,1,0:T(8,128)(2,1)} %bitcast.16), calls=%async_computation.1 | async-start | bytes 2097152 | tf_op jit(solution)/shard_map/all_to_all | solution.py:242
  136.2 1.9 copy-start.4
  138.1 1.2 copy-start.7
  160.7 1.7 copy-start.5
  164.3 1.0 copy-start.1
  165.3 81.4 %all-to-all-start.3 = ((bf16[32,3,128,128]{3,2,1,0:T(8,128)(2,1)}), bf16[32,3,128,128]{3,2,1,0:T(8,128)(2,1)S(1)}, u32[]{:S(2)}, u32[]{:S(2)}) async-start(bf16[32,3,128,128]{3,2,1,0:T(8,128)(2,1)} %copy-done.5), calls=%async_computation.3 | async-start | bytes 6291456 | tf_op jit(solution)/shard_map/all_to_all | solution.py:242
  173.1 1.2 copy-start.2

commit v3 on v2

--- a/solution.py
+++ b/solution.py
@@ -14,9 +14,9 @@
 SLOTS = 12
 SCALE = 1.0 / math.sqrt(HEAD_DIM)
 VERY_LOW = -1e30
-PAIRS_PER_STEP = 2
+PAIRS_PER_STEP = 8
 HEADS_PER_STEP = 16
-VMEM_LIMIT = 40 << 20
+VMEM_LIMIT = 30 << 20
 
 f32 = jnp.float32
 bf16 = jnp.bfloat16
@@ -97,10 +97,13 @@
                 )
 
 
-def pair_forward(load_ref, residue_ref, offsets_ref, qkv_ref, weights_ref, o_ref, pair, slot):
+def pair_scores(load_ref, qkv_ref, pair):
     q_diag = side_by_side(pair_queries(qkv_ref, pair))
     keys = listed_pair(qkv_ref, load_ref, 2 * pair, 1)
-    scores = lax.dot_general(keys, q_diag, NT, preferred_element_type=f32)
+    return lax.dot_general(keys, q_diag, NT, preferred_element_type=f32)
+
+
+def pair_weights(residue_ref, offsets_ref, scores, pair):
     residue = residue_ref[pair]
     masked = [
         jnp.where(
@@ -119,43 +122,38 @@
     for part in expos[1:]:
         total = total + part
     inverse = 1.0 / jnp.sum(total, axis=0, keepdims=True)
-    weights_t = jnp.concatenate([(part * inverse).astype(bf16) for part in expos], 0)
-    weights_ref[slot] = weights_t
-    o_ref[pair] = rows_of_pair(weights_t, qkv_ref, load_ref, pair, 2).astype(bf16)
-
-
-def pair_backward(
-    load_ref, store_ref, weights_ref, qkv_ref, g_ref, o_ref, grads_ref, k_sum, v_sum, pair, slot
-):
-    grads = g_ref[pair]
-    delta = jnp.sum((grads.astype(f32) * o_ref[pair].astype(f32)).T, axis=0, keepdims=True)
-    g_diag = side_by_side(grads)
-    q_diag = side_by_side(pair_queries(qkv_ref, pair))
+    return jnp.concatenate([(part * inverse).astype(bf16) for part in expos], 0)
+
+
+def pair_dweights(load_ref, qkv_ref, grads, pair):
     values = listed_pair(qkv_ref, load_ref, 2 * pair, 2)
-    dweights = lax.dot_general(values, g_diag, NT, preferred_element_type=f32)
-    weights_t = weights_ref[slot]
-    dscores = (weights_t.astype(f32) * (dweights - delta)).astype(bf16)
-    add_to_listed(
-        v_sum,
-        lax.dot_general(weights_t, g_diag, NN, preferred_element_type=f32),
-        store_ref,
-        2 * pair,
-    )
-    add_to_listed(
-        k_sum,
-        lax.dot_general(dscores, q_diag, NN, preferred_element_type=f32),
-        store_ref,
-        2 * pair,
-    )
-    grads_ref[pair, 0] = (rows_of_pair(dscores, qkv_ref, load_ref, pair, 1) * SCALE).astype(bf16)
+    return lax.dot_general(values, side_by_side(grads), NT, preferred_element_type=f32)
+
+
+def pair_dscores(weights_t, dweights, grads, outs):
+    delta = jnp.sum((grads.astype(f32) * outs.astype(f32)).T, axis=0, keepdims=True)
+    return (weights_t.astype(f32) * (dweights - delta)).astype(bf16)
+
+
+def staggered(number, stages):
+    for step in range(number + len(stages) - 1):
+        for k in range(len(stages)):
+            if 0 <= step - k < number:
+                stages[k](step - k)
 
 
 SCALARS = pl.BlockSpec(memory_space=pltpu.SMEM)
+IN_VMEM = pl.BlockSpec(memory_space=pltpu.VMEM)
 
 
 def resident(shape):
     zeros = (0,) * len(shape)
     return pl.BlockSpec(shape, lambda step: zeros, pipeline_mode=pl.Buffered(1))
+
+
+def per_step(shape):
+    zeros = (0,) * (len(shape) - 1)
+    return pl.BlockSpec((PAIRS_PER_STEP,) + shape[1:], lambda step: (step,) + zeros)
 
 
 def head_forward(qkv, tables):
@@ -165,23 +163,33 @@
     out_shape = (pairs, PAIR, HEAD_DIM)
 
     def body(load_ref, residue_ref, offsets_ref, qkv_ref, weights_ref, o_ref):
-        for u in range(PAIRS_PER_STEP):
-            pair = pl.program_id(0) * PAIRS_PER_STEP + u
-            pair_forward(
-                load_ref, residue_ref, offsets_ref, qkv_ref, weights_ref, o_ref, pair, u
-            )
+        first = pl.program_id(0) * PAIRS_PER_STEP
+        held = {}
+
+        def scores(u):
+            held[u] = pair_scores(load_ref, qkv_ref, first + u)
+
+        def softmax(u):
+            held[u] = pair_weights(residue_ref, offsets_ref, held[u], first + u)
+            weights_ref[u] = held[u]
+
+        def attend(u):
+            out = rows_of_pair(held.pop(u), qkv_ref, load_ref, first + u, 2)
+            o_ref[u] = out.astype(bf16)
+
+        staggered(PAIRS_PER_STEP, (scores, softmax, attend))
 
     return pl.pallas_call(
         body,
         grid=(pairs // PAIRS_PER_STEP,),
-        in_specs=[SCALARS] + [resident(x.shape) for x in (residue, offsets, qkv)],
+        in_specs=[SCALARS, resident(residue.shape), resident(offsets.shape), IN_VMEM],
         out_specs=[
-            pl.BlockSpec((PAIRS_PER_STEP,) + weights_shape[1:], lambda step: (step, 0, 0)),
-            resident(out_shape),
+            per_step(weights_shape),
+            per_step(out_shape),
         ],
         out_shape=[
             pltpu.HBM(weights_shape, bf16),
-            jax.ShapeDtypeStruct(out_shape, bf16),
+            pltpu.HBM(out_shape, bf16),
         ],
         cost_estimate=pl.CostEstimate(
             flops=20_000_000_000, transcendentals=3_000_000, bytes_accessed=10_000_000
@@ -205,12 +213,29 @@
             k_sum[...] = jnp.zeros(k_sum.shape, f32)
             v_sum[...] = jnp.zeros(v_sum.shape, f32)
 
-        for u in range(PAIRS_PER_STEP):
-            pair = pl.program_id(0) * PAIRS_PER_STEP + u
-            pair_backward(
-                load_ref, store_ref, weights_ref, qkv_ref, g_ref, o_ref, grads_ref,
-                k_sum, v_sum, pair, u,
+        first = pl.program_id(0) * PAIRS_PER_STEP
+        held = {}
+
+        def dweights(u):
+            held[u] = pair_dweights(load_ref, qkv_ref, g_ref[u], first + u)
+
+        def dscores(u):
+            grads = g_ref[u]
+            weights_t = weights_ref[u]
+            held[u] = pair_dscores(weights_t, held[u], grads, o_ref[u])
+            parts = lax.dot_general(
+                weights_t, side_by_side(grads), NN, preferred_element_type=f32
             )
+            add_to_listed(v_sum, parts, store_ref, 2 * (first + u))
+
+        def dqk(u):
+            q_diag = side_by_side(pair_queries(qkv_ref, first + u))
+            parts = lax.dot_general(held[u], q_diag, NN, preferred_element_type=f32)
+            add_to_listed(k_sum, parts, store_ref, 2 * (first + u))
+            out = rows_of_pair(held.pop(u), qkv_ref, load_ref, first + u, 1)
+            grads_ref[first + u, 0] = (out * SCALE).astype(bf16)
+
+        staggered(PAIRS_PER_STEP, (dweights, dscores, dqk))
 
         @pl.when(pl.program_id(0) == pl.num_programs(0) - 1)
         def _():
@@ -224,9 +249,11 @@
         in_specs=[
             SCALARS,
             SCALARS,
-            pl.BlockSpec((PAIRS_PER_STEP, SLOTS * BLOCK, PAIR), lambda step: (step, 0, 0)),
-        ]
-        + [resident(x.shape) for x in (qkv, g, o)],
+            per_step(weights.shape),
+            IN_VMEM,
+            per_step(g.shape),
+            per_step(o.shape),
+        ],
         out_specs=resident(grads_shape),
         out_shape=jax.ShapeDtypeStruct(grads_shape, bf16),
         scratch_shapes=[pltpu.VMEM((blocks + 1, BLOCK, HEAD_DIM), f32)] * 2,
@@ -235,7 +262,7 @@
         ),
         compiler_params=pltpu.CompilerParams(vmem_limit_bytes=VMEM_LIMIT),
         name="head_backward",
-    )(load, store, weights, qkv, g, o)
+    )(load, store, in_hbm(weights), qkv, in_hbm(g), in_hbm(o))
 
 
 def exchange(by_device):
@@ -298,11 +325,12 @@
         lax.dynamic_index_in_dim(dilation, my_head, 0, keepdims=False),
     )
     qkv = exchange(pack_heads(queries, keys, values)).reshape(-1, BLOCK, HEAD_DIM)
-    g = exchange(pack_heads(out_grad)).reshape(-1, PAIR, HEAD_DIM)
+    packed_grad, tables = lax.optimization_barrier((pack_heads(out_grad), tables))
+    g = exchange(packed_grad).reshape(-1, PAIR, HEAD_DIM)
     weights, o = head_forward(qkv, tables)
     attended = exchange(o[:, None])
     grads = exchange(head_backward(qkv, g, o, weights, tables))
-    return tuple(unpack_heads(attended)) + tuple(unpack_heads(grads))
+    return tuple(unpack_heads(in_hbm(attended))) + tuple(unpack_heads(grads))
 
 
 def solution(mesh):

time: 249 us -> 240 us (0.964)
  waiting for transfers between devices: 142 us -> 161 us
  Pallas kernels: 52.8 us -> 37.9 us
  starting transfers between devices: 35.1 us -> 27.6 us
  local copies, waits for them, and re-layouts: 15 us -> 8.55 us
    all_to_all x4, waiting for transfers between devices: 142 us -> 161 us  [exchange(): lax.all_to_all(by_device, 'seq', split_axis=0, concat_axis=0, tiled=True)]
    pallas_call x1, Pallas kernels: 22.8 us -> 10.9 us  [head_forward(): pl.pallas_call(body, grid=(pairs // PAIRS_PER_STEP,), in_specs=[SCALARS,...]
    all_to_all x4, starting transfers between devices: 35.1 us -> 27.6 us  [exchange(): lax.all_to_all(by_device, 'seq', split_axis=0, concat_axis=0, tiled=True)]
    unnamed x18 -> x10, local copies, waits for them, and re-layouts: 7.93 us -> 2.61 us
    pallas_call x1, Pallas kernels: 21.4 us -> 17.4 us  [head_backward(): pl.pallas_call(body, grid=(pairs // PAIRS_PER_STEP,), in_specs=[SCALARS,...]
  transfers between devices with their start and end apart: 4 -> 4, of which waited for: 3 -> 4; matrix products, arithmetic and copies ran while one was open for 4% -> 4% of each run, Pallas kernels for 19% -> 14%
where the time goes in v3:
time: 240 us; the launch traced here: 239 us
  waiting for transfers between devices  161 us (67%)
  Pallas kernels  37.9 us (16%)
  starting transfers between devices  27.6 us (12%)
  local copies, waits for them, and re-layouts  8.55 us (4%)
  other arithmetic  2.43 us (1%)
    all_to_all x4, waiting for transfers between devices, exchange(): lax.all_to_all(by_device, 'seq', split_axis=0, concat_axis=0, tiled=True)  161 us
    all_to_all x4, starting transfers between devices, exchange(): lax.all_to_all(by_device, 'seq', split_axis=0, concat_axis=0, tiled=True)  27.6 us
    pallas_call x1, Pallas kernels, head_backward(): pl.pallas_call(body, grid=(pairs // PAIRS_PER_STEP,), in_specs=[SCALARS,...  17.4 us
    pallas_call x1, Pallas kernels, head_forward(): pl.pallas_call(body, grid=(pairs // PAIRS_PER_STEP,), in_specs=[SCALARS,...  10.9 us
    pallas_call x2, Pallas kernels, pack_heads(): pl.pallas_call(body, grid=(width // HEAD_DIM // HEADS_PER_STEP,), in_spec...  5.44 us
  transfers between devices with their start and end apart: 4, of which 4 were waited for; matrix products, arithmetic and copies ran while one was open for 4% of the time, Pallas kernels for 14%

profile of v3, /device:TPU:2, one launch (start us, length us, event | category | flops | bytes accessed | tf_op | source)
XLA Modules:
  0.0 239.3 jit_solution(11203947863069265304)
XLA Ops:
  0.6 3.3 %pack_heads.3 = bf16[32,3,128,128]{3,2,1,0:T(8,128)(2,1)} custom-call(bf16[128,4096]{1,0:T(8,128)(2,1)} %refs_0_.3, bf16[128,4096]{1,0:T(8,128)(2,1)} %refs_1_.1, bf16[128,4096]{1,0:T(8,128)(2,1)} %refs_2_.1), custom_call_target="tpu_custom_call" | custom-call | tf_op jit(solution)/shard_map/pack_heads/pallas_call | solution.py:285
  4.0 11.6 %all-to-all-start = ((bf16[32,3,128,128]{3,2,1,0:T(8,128)(2,1)}), bf16[32,3,128,128]{3,2,1,0:T(8,128)(2,1)S(1)}, u32[]{:S(2)}, u32[]{:S(2)}) async-start(bf16[32,3,128,128]{3,2,1,0:T(8,128)(2,1)} %pack_heads.3), calls=%async_computation | async-start | bytes 6291456 | tf_op jit(solution)/shard_map/all_to_all | solution.py:269
  15.6 0.6 dynamic_slice.9
  17.5 0.7 copy.25
  18.5 2.0 fusion.6
  20.5 1.1 copy.28
  21.6 1.2 broadcast_in_dim.26
  22.8 1.2 reshape.204
  24.2 2.1 pack_heads.2
  26.3 0.7 pad.4.residue_ref
  27.0 0.4 fusion.10
  27.5 62.8 %all-to-all-done = bf16[32,3,128,128]{3,2,1,0:T(8,128)(2,1)S(1)} async-done(((bf16[32,3,128,128]{3,2,1,0:T(8,128)(2,1)}), bf16[32,3,128,128]{3,2,1,0:T(8,128)(2,1)S(1)}, u32[]{:S(2)}, u32[]{:S(2)}) %all-to-all-start) | async-done | bytes 3145760 | tf_op jit(solution)/shard_map/all_to_all | solution.py:269
  90.3 5.9 %all-to-all-start.2 = ((bf16[32,1,128,128]{3,2,1,0:T(8,128)(2,1)}), bf16[32,1,128,128]{3,2,1,0:T(8,128)(2,1)}, u32[]{:S(2)}, u32[]{:S(2)}) async-start(bf16[32,1,128,128]{3,2,1,0:T(8,128)(2,1)} %pack_heads.2), calls=%async_computation.2 | async-start | bytes 2097152 | tf_op jit(solution)/shard_map/all_to_all | solution.py:269
  96.2 0.9 copy-done.2
  97.1 10.9 %head_forward.1 = (bf16[32,768,128]{2,1,0:T(8,128)(2,1)}, bf16[32,128,128]{2,1,0:T(8,128)(2,1)}) custom-call(s32[64,12]{1,0:T(8,128)S(1)} %get-tuple-element.14.load_ref, s32[32,16,128]{2,1,0:T(8,128)S(1)} %copy-done.2, s32[2,64,128]{2,1,0:T(8,128)S(1)} %pad_add_fusion.offsets_ref, bf16[192,64,128]{2,1,0:T(8,128)(2,1)S(1)} %bitcast.14), custom_call_target="tpu_custom_call" | custom-call | flops 20000000000 | bytes 10000000 | tf_op jit(solution)/shard_map/head_forward/pallas_call | solution.py:182
  108.0 16.7 %all-to-all-done.2 = bf16[32,1,128,128]{3,2,1,0:T(8,128)(2,1)} async-done(((bf16[32,1,128,128]{3,2,1,0:T(8,128)(2,1)}), bf16[32,1,128,128]{3,2,1,0:T(8,128)(2,1)}, u32[]{:S(2)}, u32[]{:S(2)}) %all-to-all-start.2) | async-done | bytes 1048608 | tf_op jit(solution)/shard_map/all_to_all | solution.py:269
  124.8 5.1 %all-to-all-start.1 = ((bf16[32,1,128,128]{3,2,1,0:T(8,128)(2,1)}), bf16[32,1,128,128]{3,2,1,0:T(8,128)(2,1)}, u32[]{:S(2)}, u32[]{:S(2)}) async-start(bf16[32,1,128,128]{3,2,1,0:T(8,128)(2,1)} %bitcast.16), calls=%async_computation.1 | async-start | bytes 2097152 | tf_op jit(solution)/shard_map/all_to_all | solution.py:269
  129.9 17.4 %head_backward.1 = bf16[32,3,128,128]{3,2,1,0:T(8,128)(2,1)S(1)} custom-call(s32[64,12]{1,0:T(8,128)S(1)} %get-tuple-element.14.load_ref, s32[64,12]{1,0:T(8,128)S(1)} %get-tuple-element.18.store_ref, bf16[32,768,128]{2,1,0:T(8,128)(2,1)} %get-tuple-element.19.weights_ref, bf16[192,64,128]{2,1,0:T(8,128)(2,1)S(1)} %bitcast.15, ...), custom_call_target="tpu_custom_call" | custom-call | flops 24000000000 | bytes 16000000 | tf_op jit(solution)/shard_map/head_backward/pallas_call | solution.py:246
  147.3 1.6 copy-done.1
  148.9 9.2 %all-to-all-done.1.packed_ref = bf16[32,1,128,128]{3,2,1,0:T(8,128)(2,1)} async-done(((bf16[32,1,128,128]{3,2,1,0:T(8,128)(2,1)}), bf16[32,1,128,128]{3,2,1,0:T(8,128)(2,1)}, u32[]{:S(2)}, u32[]{:S(2)}) %all-to-all-start.1) | async-done | bytes 1048608 | tf_op jit(solution)/shard_map/all_to_all | solution.py:269
  158.2 4.9 %all-to-all-start.3 = ((bf16[32,3,128,128]{3,2,1,0:T(8,128)(2,1)}), bf16[32,3,128,128]{3,2,1,0:T(8,128)(2,1)S(1)}, u32[]{:S(2)}, u32[]{:S(2)}) async-start(bf16[32,3,128,128]{3,2,1,0:T(8,128)(2,1)} %copy-done.1), calls=%async_computation.3 | async-start | bytes 6291456 | tf_op jit(solution)/shard_map/all_to_all | solution.py:269
  163.1 2.2 unpack_heads.2
  165.2 72.0 %all-to-all-done.3.packed_ref = bf16[32,3,128,128]{3,2,1,0:T(8,128)(2,1)S(1)} async-done(((bf16[32,3,128,128]{3,2,1,0:T(8,128)(2,1)}), bf16[32,3,128,128]{3,2,1,0:T(8,128)(2,1)S(1)}, u32[]{:S(2)}, u32[]{:S(2)}) %all-to-all-start.3) | async-done | bytes 3145760 | tf_op jit(solution)/shard_map/all_to_all | solution.py:269
  237.2 2.1 unpack_heads.3
  (20 shorter events, 0.5 us)
Async XLA Ops:
  0.6 16.9 %copy-start = (s32[32,64,12]{1,0,2:T(8,128)S(1)}, s32[32,64,12]{1,0,2:T(8,128)}, u32[]{:S(2)}) copy-start(s32[32,64,12]{1,0,2:T(8,128)} %param.10) | copy-start | bytes 294916
  4.0 11.6 %copy-start.4 = (s32[32]{0:T(128)S(1)}, s32[32]{0:T(128)}, u32[]{:S(2)}) copy-start(s32[32]{0:T(128)} %param.11) | copy-start | bytes 388
  4.0 86.3 %all-to-all-start = ((bf16[32,3,128,128]{3,2,1,0:T(8,128)(2,1)}), bf16[32,3,128,128]{3,2,1,0:T(8,128)(2,1)S(1)}, u32[]{:S(2)}, u32[]{:S(2)}) async-start(bf16[32,3,128,128]{3,2,1,0:T(8,128)(2,1)} %pack_heads.3), calls=%async_computation | async-start | bytes 6291456 | tf_op jit(solution)/shard_map/all_to_all | solution.py:269
  24.1 3.4 %copy-start.3 = (s32[1,64,12]{2,1,0:T(8,128)S(1)}, s32[1,64,12]{2,1,0:T(8,128)}, u32[]{:S(2)}) copy-start(s32[1,64,12]{2,1,0:T(8,128)} %copy.25) | copy-start | bytes 9220
  90.3 34.5 %all-to-all-start.2 = ((bf16[32,1,128,128]{3,2,1,0:T(8,128)(2,1)}), bf16[32,1,128,128]{3,2,1,0:T(8,128)(2,1)}, u32[]{:S(2)}, u32[]{:S(2)}) async-start(bf16[32,1,128,128]{3,2,1,0:T(8,128)(2,1)} %pack_heads.2), calls=%async_computation.2 | async-start | bytes 2097152 | tf_op jit(solution)/shard_map/all_to_all | solution.py:269
  96.2 1.0 copy-start.2
  124.8 33.4 %all-to-all-start.1 = ((bf16[32,1,128,128]{3,2,1,0:T(8,128)(2,1)}), bf16[32,1,128,128]{3,2,1,0:T(8,128)(2,1)}, u32[]{:S(2)}, u32[]{:S(2)}) async-start(bf16[32,1,128,128]{3,2,1,0:T(8,128)(2,1)} %bitcast.16), calls=%async_computation.1 | async-start | bytes 2097152 | tf_op jit(solution)/shard_map/all_to_all | solution.py:269
  147.3 1.7 copy-start.1
  158.2 79.0 %all-to-all-start.3 = ((bf16[32,3,128,128]{3,2,1,0:T(8,128)(2,1)}), bf16[32,3,128,128]{3,2,1,0:T(8,128)(2,1)S(1)}, u32[]{:S(2)}, u32[]{:S(2)}) async-start(bf16[32,3,128,128]{3,2,1,0:T(8,128)(2,1)} %copy-done.1), calls=%async_computation.3 | async-start | bytes 6291456 | tf_op jit(solution)/shard_map/all_to_all | solution.py:269

commit v4 on v3

--- a/solution.py
+++ b/solution.py
@@ -1,3 +1,4 @@
+import functools
 import math
 
 import jax
@@ -29,7 +30,6 @@
     ids = jnp.arange(blocks, dtype=jnp.int32)[:, None]
     valid = lists >= 0
     listed_block = jnp.maximum(lists, 0)
-    load = listed_block // 2 * 6 + listed_block % 2
     store = jnp.where(valid, lists, blocks)
     residue = jnp.where(valid, jnp.mod((listed_block - ids) * BLOCK, spacing), -1)
     residue = residue.reshape(blocks // 2, 2, SLOTS).transpose(0, 2, 1)
@@ -39,7 +39,7 @@
     key_at = lax.broadcasted_iota(jnp.int32, (BLOCK, PAIR), 0)
     query_at = lax.broadcasted_iota(jnp.int32, (BLOCK, PAIR), 1) % BLOCK
     offsets = jnp.mod(query_at - key_at, spacing)
-    return load, store, residue, jnp.stack([jnp.where(query_at >= key_at, offsets, -2), offsets])
+    return listed_block, store, residue, jnp.stack([jnp.where(query_at >= key_at, offsets, -2), offsets])
 
 
 def side_by_side(rows):
@@ -53,27 +53,36 @@
     )
 
 
-def listed(packed_ref, load_ref, block, array):
-    return [packed_ref[load_ref[block, s] + 2 * array] for s in range(SLOTS)]
-
-
-def listed_pair(packed_ref, load_ref, first, array):
-    left = listed(packed_ref, load_ref, first, array)
-    right = listed(packed_ref, load_ref, first + 1, array)
+class Packed:
+    def __init__(self, source, number, place):
+        self.source, self.number, self.place = source, number, place
+
+    def positions(self, blocks):
+        return blocks // 2 * (2 * self.number) + 2 * self.place + blocks % 2
+
+
+def listed(packed_ref, load_ref, block):
+    return [packed_ref[load_ref[block, s]] for s in range(SLOTS)]
+
+
+def listed_pair(packed_ref, load_ref, first):
+    left = listed(packed_ref, load_ref, first)
+    right = listed(packed_ref, load_ref, first + 1)
     return jnp.concatenate(
         [jnp.concatenate([a, b], 1) for a, b in zip(left, right)], 0
     )
 
 
-def pair_queries(packed_ref, pair):
-    return packed_ref[pl.ds(6 * pair, 2)].reshape(PAIR, HEAD_DIM)
-
-
-def rows_of_pair(weights_t, packed_ref, load_ref, pair, array):
+def pair_queries(packed_ref, layout, pair):
+    start = 2 * layout.number * pair + 2 * layout.place
+    return packed_ref[pl.ds(start, 2)].reshape(PAIR, HEAD_DIM)
+
+
+def rows_of_pair(weights_t, packed_ref, load_ref, pair):
     weights = weights_t.T
     outs = []
     for half in range(2):
-        rows = jnp.concatenate(listed(packed_ref, load_ref, 2 * pair + half, array), 0)
+        rows = jnp.concatenate(listed(packed_ref, load_ref, 2 * pair + half), 0)
         outs.append(
             lax.dot_general(
                 weights[half * BLOCK : (half + 1) * BLOCK], rows, NN, preferred_element_type=f32
@@ -97,9 +106,9 @@
                 )
 
 
-def pair_scores(load_ref, qkv_ref, pair):
-    q_diag = side_by_side(pair_queries(qkv_ref, pair))
-    keys = listed_pair(qkv_ref, load_ref, 2 * pair, 1)
+def pair_scores(load_ref, q_rows, keys_ref, pair):
+    q_diag = side_by_side(q_rows)
+    keys = listed_pair(keys_ref, load_ref, 2 * pair)
     return lax.dot_general(keys, q_diag, NT, preferred_element_type=f32)
 
 
@@ -125,8 +134,8 @@
     return jnp.concatenate([(part * inverse).astype(bf16) for part in expos], 0)
 
 
-def pair_dweights(load_ref, qkv_ref, grads, pair):
-    values = listed_pair(qkv_ref, load_ref, 2 * pair, 2)
+def pair_dweights(load_ref, values_ref, grads, pair):
+    values = listed_pair(values_ref, load_ref, 2 * pair)
     return lax.dot_general(values, side_by_side(grads), NT, preferred_element_type=f32)
 
 
@@ -156,25 +165,29 @@
     return pl.BlockSpec((PAIRS_PER_STEP,) + shape[1:], lambda step: (step,) + zeros)
 
 
-def head_forward(qkv, tables):
-    load, _, residue, offsets = tables
+def head_forward(packed, layouts, tables):
+    k_load, v_load, _, residue, offsets = tables
+    q_at, k_at, v_at = layouts
     pairs = residue.shape[0]
     weights_shape = (pairs, SLOTS * BLOCK, PAIR)
     out_shape = (pairs, PAIR, HEAD_DIM)
 
-    def body(load_ref, residue_ref, offsets_ref, qkv_ref, weights_ref, o_ref):
+    def body(k_load_ref, v_load_ref, residue_ref, offsets_ref, *refs):
+        packed_refs, (weights_ref, o_ref) = refs[: len(packed)], refs[len(packed) :]
+        k_ref, v_ref = packed_refs[k_at.source], packed_refs[v_at.source]
         first = pl.program_id(0) * PAIRS_PER_STEP
         held = {}
 
         def scores(u):
-            held[u] = pair_scores(load_ref, qkv_ref, first + u)
+            q_rows = pair_queries(packed_refs[q_at.source], q_at, first + u)
+            held[u] = pair_scores(k_load_ref, q_rows, k_ref, first + u)
 
         def softmax(u):
             held[u] = pair_weights(residue_ref, offsets_ref, held[u], first + u)
             weights_ref[u] = held[u]
 
         def attend(u):
-            out = rows_of_pair(held.pop(u), qkv_ref, load_ref, first + u, 2)
+            out = rows_of_pair(held.pop(u), v_ref, v_load_ref, first + u)
             o_ref[u] = out.astype(bf16)
 
         staggered(PAIRS_PER_STEP, (scores, softmax, attend))
@@ -182,7 +195,8 @@
     return pl.pallas_call(
         body,
         grid=(pairs // PAIRS_PER_STEP,),
-        in_specs=[SCALARS, resident(residue.shape), resident(offsets.shape), IN_VMEM],
+        in_specs=[SCALARS, SCALARS, resident(residue.shape), resident(offsets.shape)]
+        + [IN_VMEM] * len(packed),
         out_specs=[
             per_step(weights_shape),
             per_step(out_shape),
@@ -196,18 +210,20 @@
         ),
         compiler_params=pltpu.CompilerParams(vmem_limit_bytes=VMEM_LIMIT),
         name="head_forward",
-    )(load, residue, offsets, qkv)
-
-
-def head_backward(qkv, g, o, weights, tables):
-    load, store, _, _ = tables
+    )(k_load, v_load, residue, offsets, *packed)
+
+
+def head_backward(packed, layouts, g, o, weights, tables):
+    k_load, v_load, store, _, _ = tables
+    q_at, k_at, v_at = layouts
     pairs = g.shape[0]
     blocks = 2 * pairs
     grads_shape = (pairs, 3, PAIR, HEAD_DIM)
 
-    def body(
-        load_ref, store_ref, weights_ref, qkv_ref, g_ref, o_ref, grads_ref, k_sum, v_sum
-    ):
+    def body(k_load_ref, v_load_ref, store_ref, weights_ref, g_ref, o_ref, *refs):
+        packed_refs, (grads_ref, k_sum, v_sum) = refs[: len(packed)], refs[len(packed) :]
+        k_ref, v_ref = packed_refs[k_at.source], packed_refs[v_at.source]
+
         @pl.when(pl.program_id(0) == 0)
         def _():
             k_sum[...] = jnp.zeros(k_sum.shape, f32)
@@ -217,7 +233,7 @@
         held = {}
 
         def dweights(u):
-            held[u] = pair_dweights(load_ref, qkv_ref, g_ref[u], first + u)
+            held[u] = pair_dweights(v_load_ref, v_ref, g_ref[u], first + u)
 
         def dscores(u):
             grads = g_ref[u]
@@ -229,10 +245,11 @@
             add_to_listed(v_sum, parts, store_ref, 2 * (first + u))
 
         def dqk(u):
-            q_diag = side_by_side(pair_queries(qkv_ref, first + u))
+            q_rows = pair_queries(packed_refs[q_at.source], q_at, first + u)
+            q_diag = side_by_side(q_rows)
             parts = lax.dot_general(held[u], q_diag, NN, preferred_element_type=f32)
             add_to_listed(k_sum, parts, store_ref, 2 * (first + u))
-            out = rows_of_pair(held.pop(u), qkv_ref, load_ref, first + u, 1)
+            out = rows_of_pair(held.pop(u), k_ref, k_load_ref, first + u)
             grads_ref[first + u, 0] = (out * SCALE).astype(bf16)
 
         staggered(PAIRS_PER_STEP, (dweights, dscores, dqk))
@@ -249,11 +266,12 @@
         in_specs=[
             SCALARS,
             SCALARS,
+            SCALARS,
             per_step(weights.shape),
-            IN_VMEM,
             per_step(g.shape),
             per_step(o.shape),
-        ],
+        ]
+        + [IN_VMEM] * len(packed),
         out_specs=resident(grads_shape),
         out_shape=jax.ShapeDtypeStruct(grads_shape, bf16),
         scratch_shapes=[pltpu.VMEM((blocks + 1, BLOCK, HEAD_DIM), f32)] * 2,
@@ -262,7 +280,7 @@
         ),
         compiler_params=pltpu.CompilerParams(vmem_limit_bytes=VMEM_LIMIT),
         name="head_backward",
-    )(load, store, in_hbm(weights), qkv, in_hbm(g), in_hbm(o))
+    )(k_load, v_load, store, in_hbm(weights), in_hbm(g), in_hbm(o), *packed)
 
 
 def exchange(by_device):
@@ -318,19 +336,44 @@
     )(packed)
 
 
-def local(queries, keys, values, out_grad, key_blocks, dilation):
+def after(first, *later):
+    return lax.optimization_barrier((first,) + later)[1:]
+
+
+def one_head(portions, layouts, queries, keys, values, out_grad, key_blocks, dilation):
+    arrays = (queries, keys, values)
+    packed = []
+    for portion in portions:
+        sources = [arrays[i] for i in portion]
+        if packed:
+            sources = after(packed[-1][:1, :1, :1, :1], *sources)
+        packed.append(exchange(pack_heads(*sources)))
+    packed = [x.reshape(-1, BLOCK, HEAD_DIM) for x in packed]
     my_head = lax.axis_index("seq")
-    tables = index_tables(
+    lists, store, residue, offsets = index_tables(
         lax.dynamic_index_in_dim(key_blocks, my_head, 0, keepdims=False),
         lax.dynamic_index_in_dim(dilation, my_head, 0, keepdims=False),
     )
-    qkv = exchange(pack_heads(queries, keys, values)).reshape(-1, BLOCK, HEAD_DIM)
+    tables = (layouts[1].positions(lists), layouts[2].positions(lists), store, residue, offsets)
     packed_grad, tables = lax.optimization_barrier((pack_heads(out_grad), tables))
     g = exchange(packed_grad).reshape(-1, PAIR, HEAD_DIM)
-    weights, o = head_forward(qkv, tables)
+    weights, o = head_forward(packed, layouts, tables)
     attended = exchange(o[:, None])
-    grads = exchange(head_backward(qkv, g, o, weights, tables))
+    grads = exchange(head_backward(packed, layouts, g, o, weights, tables))
     return tuple(unpack_heads(in_hbm(attended))) + tuple(unpack_heads(grads))
+
+
+ALL_AT_ONCE = functools.partial(
+    one_head, ((0, 1, 2),), (Packed(0, 3, 0), Packed(0, 3, 1), Packed(0, 3, 2))
+)
+VALUES_FIRST = functools.partial(
+    one_head, ((2,), (0, 1)), (Packed(1, 2, 0), Packed(1, 2, 1), Packed(0, 1, 0))
+)
+
+
+def local(*arguments):
+    odd = lax.axis_index("batch") % 2
+    return lax.cond(odd == 0, ALL_AT_ONCE, VALUES_FIRST, *arguments)
 
 
 def solution(mesh):

time: 240 us -> 230 us (0.958)
  the two profiles are of different devices: /device:TPU:2 before, /device:TPU:1 now
where the time goes in v4:
time: 230 us; the launch traced here: 229 us
  waiting for transfers between devices  133 us (58%)
  Pallas kernels  40.5 us (18%)
  starting transfers between devices  39 us (17%)
  local copies, waits for them, and re-layouts  9.58 us (4%)
  other arithmetic  4.71 us (2%)
    all_to_all x5, waiting for transfers between devices, exchange(): lax.all_to_all(by_device, 'seq', split_axis=0, concat_axis=0, tiled=True)  133 us
    all_to_all x5, starting transfers between devices, exchange(): lax.all_to_all(by_device, 'seq', split_axis=0, concat_axis=0, tiled=True)  39 us
    pallas_call x1, Pallas kernels, head_backward(): pl.pallas_call(body, grid=(pairs // PAIRS_PER_STEP,), in_specs=[SCALARS,...  18 us
    pallas_call x1, Pallas kernels, head_forward(): pl.pallas_call(body, grid=(pairs // PAIRS_PER_STEP,), in_specs=[SCALARS,...  11.4 us
    pallas_call x3, Pallas kernels, pack_heads(): pl.pallas_call(body, grid=(width // HEAD_DIM // HEADS_PER_STEP,), in_spec...  6.97 us
  transfers between devices with their start and end apart: 5, of which 5 were waited for; matrix products, arithmetic and copies ran while one was open for 5% of the time, Pallas kernels for 16%

profile of v4, /device:TPU:1, one launch (start us, length us, event | category | flops | bytes accessed | tf_op | source)
XLA Modules:
  0.0 229.2 jit_solution(15621083209380024409)
XLA Ops:
  0.6 228.6 %conditional.1 = (bf16[128,4096]{1,0:T(8,128)(2,1)}, bf16[128,4096]{1,0:T(8,128)(2,1)}, bf16[128,4096]{1,0:T(8,128)(2,1)}, bf16[128,4096]{1,0:T(8,128)(2,1)}) conditional(s32[]{:T(128)} %convert_element_type.3, (bf16[128,4096]{1,0:T(8,128)(2,1)}, s32[32,64,12]{1,0,2:T(8,128)}, s32[32]{0:T(128)}, bf16[128,4096]{1,0:T(8,128)(2,1)}, ...), branch_computations={%region_0.1_spmd, %region_1.2_spmd} | conditional | flops 44000133120 | bytes 66045268 | solution.py:376
  0.7 2.1 pack_heads.6
  2.8 12.0 %all-to-all-start = ((bf16[32,1,128,128]{3,2,1,0:T(8,128)(2,1)}), bf16[32,1,128,128]{3,2,1,0:T(8,128)(2,1)S(1)}, u32[]{:S(2)}, u32[]{:S(2)}) async-start(bf16[32,1,128,128]{3,2,1,0:T(8,128)(2,1)} %pack_heads.6), calls=%async_computation | async-start | bytes 2097152 | tf_op jit(solution)/shard_map/cond/branch_0_fun/all_to_all | solution.py:287
  14.8 2.8 %pack_heads.7 = bf16[32,2,128,128]{3,2,1,0:T(8,128)(2,1)} custom-call(bf16[128,4096]{1,0:T(8,128)(2,1)} %get-tuple-element.34.refs_0_, bf16[128,4096]{1,0:T(8,128)(2,1)} %get-tuple-element.35.refs_1_), custom_call_target="tpu_custom_call" | custom-call | tf_op jit(solution)/shard_map/cond/branch_0_fun/pack_heads/pallas_call | solution.py:303
  17.6 20.7 %all-to-all-done = bf16[32,1,128,128]{3,2,1,0:T(8,128)(2,1)S(1)} async-done(((bf16[32,1,128,128]{3,2,1,0:T(8,128)(2,1)}), bf16[32,1,128,128]{3,2,1,0:T(8,128)(2,1)S(1)}, u32[]{:S(2)}, u32[]{:S(2)}) %all-to-all-start) | async-done | bytes 1048608 | tf_op jit(solution)/shard_map/cond/branch_0_fun/all_to_all | solution.py:287
  38.3 10.4 %all-to-all-start.1 = ((bf16[32,2,128,128]{3,2,1,0:T(8,128)(2,1)}), bf16[32,2,128,128]{3,2,1,0:T(8,128)(2,1)S(1)}, u32[]{:S(2)}, u32[]{:S(2)}) async-start(bf16[32,2,128,128]{3,2,1,0:T(8,128)(2,1)} %pack_heads.7), calls=%async_computation.1 | async-start | bytes 4194304 | tf_op jit(solution)/shard_map/cond/branch_0_fun/all_to_all | solution.py:287
  50.6 1.4 copy.30
  53.6 1.4 fusion.4
  56.0 1.5 broadcast_in_dim.35
  58.4 1.0 copy.27
  59.4 2.1 pack_heads.5
  61.9 1.4 compare_select_fusion
  63.4 23.9 %all-to-all-done.1 = bf16[32,2,128,128]{3,2,1,0:T(8,128)(2,1)S(1)} async-done(((bf16[32,2,128,128]{3,2,1,0:T(8,128)(2,1)}), bf16[32,2,128,128]{3,2,1,0:T(8,128)(2,1)S(1)}, u32[]{:S(2)}, u32[]{:S(2)}) %all-to-all-start.1) | async-done | bytes 2097184 | tf_op jit(solution)/shard_map/cond/branch_0_fun/all_to_all | solution.py:287
  87.3 6.9 %all-to-all-start.3 = ((bf16[32,1,128,128]{3,2,1,0:T(8,128)(2,1)}), bf16[32,1,128,128]{3,2,1,0:T(8,128)(2,1)}, u32[]{:S(2)}, u32[]{:S(2)}) async-start(bf16[32,1,128,128]{3,2,1,0:T(8,128)(2,1)} %pack_heads.5), calls=%async_computation.3 | async-start | bytes 2097152 | tf_op jit(solution)/shard_map/cond/branch_0_fun/all_to_all | solution.py:287
  94.9 11.4 %head_forward.2 = (bf16[32,768,128]{2,1,0:T(8,128)(2,1)}, bf16[32,128,128]{2,1,0:T(8,128)(2,1)}) custom-call(s32[64,12]{1,0:T(8,128)S(1)} %get-tuple-element.27.k_load_ref, s32[64,12]{1,0:T(8,128)S(1)} %copy-done.2, s32[32,16,128]{2,1,0:T(8,128)S(1)} %pad.5.residue_ref, s32[2,64,128]{2,1,0:T(8,128)S(1)} %pad_add_fusion.offsets_ref, ...), custom_call_target="tpu_custom_call" | custom-call | flops 20000000000 | bytes 10000000 | tf_op jit(solution)/shard_map/cond/branch_0_fun/head_forward/pallas_call | solution.py:195
  106.3 11.5 %all-to-all-done.3 = bf16[32,1,128,128]{3,2,1,0:T(8,128)(2,1)} async-done(((bf16[32,1,128,128]{3,2,1,0:T(8,128)(2,1)}), bf16[32,1,128,128]{3,2,1,0:T(8,128)(2,1)}, u32[]{:S(2)}, u32[]{:S(2)}) %all-to-all-start.3) | async-done | bytes 1048608 | tf_op jit(solution)/shard_map/cond/branch_0_fun/all_to_all | solution.py:287
  117.8 4.9 %all-to-all-start.2 = ((bf16[32,1,128,128]{3,2,1,0:T(8,128)(2,1)}), bf16[32,1,128,128]{3,2,1,0:T(8,128)(2,1)}, u32[]{:S(2)}, u32[]{:S(2)}) async-start(bf16[32,1,128,128]{3,2,1,0:T(8,128)(2,1)} %bitcast.71), calls=%async_computation.2 | async-start | bytes 2097152 | tf_op jit(solution)/shard_map/cond/branch_0_fun/all_to_all | solution.py:287
  123.5 18.0 %head_backward.2 = bf16[32,3,128,128]{3,2,1,0:T(8,128)(2,1)S(1)} custom-call(s32[64,12]{1,0:T(8,128)S(1)} %get-tuple-element.27.k_load_ref, s32[64,12]{1,0:T(8,128)S(1)} %copy-done.3, s32[64,12]{1,0:T(8,128)S(1)} %get-tuple-element.37.store_ref, bf16[32,768,128]{2,1,0:T(8,128)(2,1)} %get-tuple-element.38.weights_ref, bf16[32,128,128]{2,1,0:T(8,128)(2,1)} %bitcast.6.g_ref, ...), custom_call_target="tpu_custom_call" | custom-call | flops 24000000000 | bytes 16000000 | tf_op jit(solution)/shard_map/cond/branch_0_fun/head_backward/pallas_call | solution.py:263
  141.4 1.6 copy-done
  143.0 5.6 %all-to-all-done.2.packed_ref = bf16[32,1,128,128]{3,2,1,0:T(8,128)(2,1)} async-done(((bf16[32,1,128,128]{3,2,1,0:T(8,128)(2,1)}), bf16[32,1,128,128]{3,2,1,0:T(8,128)(2,1)}, u32[]{:S(2)}, u32[]{:S(2)}) %all-to-all-start.2) | async-done | bytes 1048608 | tf_op jit(solution)/shard_map/cond/branch_0_fun/all_to_all | solution.py:287
  148.6 4.8 %all-to-all-start.4 = ((bf16[32,3,128,128]{3,2,1,0:T(8,128)(2,1)}), bf16[32,3,128,128]{3,2,1,0:T(8,128)(2,1)S(1)}, u32[]{:S(2)}, u32[]{:S(2)}) async-start(bf16[32,3,128,128]{3,2,1,0:T(8,128)(2,1)} %copy-done), calls=%async_computation.4 | async-start | bytes 6291456 | tf_op jit(solution)/shard_map/cond/branch_0_fun/all_to_all | solution.py:287
  153.4 2.2 unpack_heads.4
  155.6 71.6 %all-to-all-done.4.packed_ref = bf16[32,3,128,128]{3,2,1,0:T(8,128)(2,1)S(1)} async-done(((bf16[32,3,128,128]{3,2,1,0:T(8,128)(2,1)}), bf16[32,3,128,128]{3,2,1,0:T(8,128)(2,1)S(1)}, u32[]{:S(2)}, u32[]{:S(2)}) %all-to-all-start.4) | async-done | bytes 3145760 | tf_op jit(solution)/shard_map/cond/branch_0_fun/all_to_all | solution.py:287
  227.1 2.1 unpack_heads.5
  (21 shorter events, 6.0 us)
Async XLA Ops:
  2.8 35.5 %all-to-all-start = ((bf16[32,1,128,128]{3,2,1,0:T(8,128)(2,1)}), bf16[32,1,128,128]{3,2,1,0:T(8,128)(2,1)S(1)}, u32[]{:S(2)}, u32[]{:S(2)}) async-start(bf16[32,1,128,128]{3,2,1,0:T(8,128)(2,1)} %pack_heads.6), calls=%async_computation | async-start | bytes 2097152 | tf_op jit(solution)/shard_map/cond/branch_0_fun/all_to_all | solution.py:287
  17.6 31.2 %copy-start.8 = (s32[32]{0:T(128)S(1)}, s32[32]{0:T(128)}, u32[]{:S(2)}) copy-start(s32[32]{0:T(128)} %get-tuple-element.26) | copy-start | bytes 388 | tf_op jit(solution)/shard_map/cond
  17.6 33.1 %copy-start.6 = (s32[32,64,12]{1,0,2:T(8,128)S(1)}, s32[32,64,12]{1,0,2:T(8,128)}, u32[]{:S(2)}) copy-start(s32[32,64,12]{1,0,2:T(8,128)} %get-tuple-element.90) | copy-start | bytes 294916 | tf_op jit(solution)/shard_map/cond
  38.3 49.0 %all-to-all-start.1 = ((bf16[32,2,128,128]{3,2,1,0:T(8,128)(2,1)}), bf16[32,2,128,128]{3,2,1,0:T(8,128)(2,1)S(1)}, u32[]{:S(2)}, u32[]{:S(2)}) async-start(bf16[32,2,128,128]{3,2,1,0:T(8,128)(2,1)} %pack_heads.7), calls=%async_computation.1 | async-start | bytes 4194304 | tf_op jit(solution)/shard_map/cond/branch_0_fun/all_to_all | solution.py:287
  87.3 30.5 %all-to-all-start.3 = ((bf16[32,1,128,128]{3,2,1,0:T(8,128)(2,1)}), bf16[32,1,128,128]{3,2,1,0:T(8,128)(2,1)}, u32[]{:S(2)}, u32[]{:S(2)}) async-start(bf16[32,1,128,128]{3,2,1,0:T(8,128)(2,1)} %pack_heads.5), calls=%async_computation.3 | async-start | bytes 2097152 | tf_op jit(solution)/shard_map/cond/branch_0_fun/all_to_all | solution.py:287
  94.2 0.8 copy-start.2
  117.8 30.8 %all-to-all-start.2 = ((bf16[32,1,128,128]{3,2,1,0:T(8,128)(2,1)}), bf16[32,1,128,128]{3,2,1,0:T(8,128)(2,1)}, u32[]{:S(2)}, u32[]{:S(2)}) async-start(bf16[32,1,128,128]{3,2,1,0:T(8,128)(2,1)} %bitcast.71), calls=%async_computation.2 | async-start | bytes 2097152 | tf_op jit(solution)/shard_map/cond/branch_0_fun/all_to_all | solution.py:287
  122.7 0.8 copy-start.3
  141.4 1.6 copy-start
  148.6 78.5 %all-to-all-start.4 = ((bf16[32,3,128,128]{3,2,1,0:T(8,128)(2,1)}), bf16[32,3,128,128]{3,2,1,0:T(8,128)(2,1)S(1)}, u32[]{:S(2)}, u32[]{:S(2)}) async-start(bf16[32,3,128,128]{3,2,1,0:T(8,128)(2,1)} %copy-done), calls=%async_computation.4 | async-start | bytes 6291456 | tf_op jit(solution)/shard_map/cond/branch_0_fun/all_to_all | solution.py:287

commit v5 on v4

--- a/solution.py
+++ b/solution.py
@@ -16,6 +16,7 @@
 SCALE = 1.0 / math.sqrt(HEAD_DIM)
 VERY_LOW = -1e30
 PAIRS_PER_STEP = 8
+PAIRS_AT_ONCE = 8
 HEADS_PER_STEP = 16
 VMEM_LIMIT = 30 << 20
 
@@ -283,6 +284,77 @@
     )(k_load, v_load, store, in_hbm(weights), in_hbm(g), in_hbm(o), *packed)
 
 
+def head_at_once(packed, layouts, tables):
+    k_load, v_load, store, residue, offsets = tables
+    q_at, k_at, v_at, g_at = layouts
+    pairs = residue.shape[0]
+    blocks = 2 * pairs
+    out_shape = (pairs, 4, PAIR, HEAD_DIM)
+
+    def body(
+        k_load_ref, v_load_ref, store_ref, residue_ref, offsets_ref, packed_ref, out_ref, k_sum, v_sum
+    ):
+        @pl.when(pl.program_id(0) == 0)
+        def _():
+            k_sum[...] = jnp.zeros(k_sum.shape, f32)
+            v_sum[...] = jnp.zeros(v_sum.shape, f32)
+
+        first = pl.program_id(0) * PAIRS_AT_ONCE
+        held = {}
+        weights = {}
+
+        def scores(u):
+            q_rows = pair_queries(packed_ref, q_at, first + u)
+            held[u] = pair_scores(k_load_ref, q_rows, packed_ref, first + u)
+
+        def softmax(u):
+            weights[u] = pair_weights(residue_ref, offsets_ref, held[u], first + u)
+            grads = pair_queries(packed_ref, g_at, first + u)
+            held[u] = pair_dweights(v_load_ref, packed_ref, grads, first + u)
+
+        def attend(u):
+            out = rows_of_pair(weights[u], packed_ref, v_load_ref, first + u).astype(bf16)
+            out_ref[first + u, 0] = out
+            grads = pair_queries(packed_ref, g_at, first + u)
+            held[u] = pair_dscores(weights[u], held[u], grads, out)
+
+        def dvalues(u):
+            grads = pair_queries(packed_ref, g_at, first + u)
+            parts = lax.dot_general(
+                weights.pop(u), side_by_side(grads), NN, preferred_element_type=f32
+            )
+            add_to_listed(v_sum, parts, store_ref, 2 * (first + u))
+
+        def dqk(u):
+            q_diag = side_by_side(pair_queries(packed_ref, q_at, first + u))
+            parts = lax.dot_general(held[u], q_diag, NN, preferred_element_type=f32)
+            add_to_listed(k_sum, parts, store_ref, 2 * (first + u))
+            out = rows_of_pair(held.pop(u), packed_ref, k_load_ref, first + u)
+            out_ref[first + u, 1] = (out * SCALE).astype(bf16)
+
+        staggered(PAIRS_AT_ONCE, (scores, softmax, attend, dvalues, dqk))
+
+        @pl.when(pl.program_id(0) == pl.num_programs(0) - 1)
+        def _():
+            by_pair = (pairs, PAIR, HEAD_DIM)
+            out_ref[:, 2] = (k_sum[:blocks] * SCALE).astype(bf16).reshape(by_pair)
+            out_ref[:, 3] = v_sum[:blocks].astype(bf16).reshape(by_pair)
+
+    return pl.pallas_call(
+        body,
+        grid=(pairs // PAIRS_AT_ONCE,),
+        in_specs=[SCALARS] * 3 + [resident(residue.shape), resident(offsets.shape), IN_VMEM],
+        out_specs=resident(out_shape),
+        out_shape=jax.ShapeDtypeStruct(out_shape, bf16),
+        scratch_shapes=[pltpu.VMEM((blocks + 1, BLOCK, HEAD_DIM), f32)] * 2,
+        cost_estimate=pl.CostEstimate(
+            flops=44_000_000_000, transcendentals=3_000_000, bytes_accessed=10_000_000
+        ),
+        compiler_params=pltpu.CompilerParams(vmem_limit_bytes=VMEM_LIMIT),
+        name="head_at_once",
+    )(k_load, v_load, store, residue, offsets, packed)
+
+
 def exchange(by_device):
     return lax.all_to_all(by_device, "seq", split_axis=0, concat_axis=0, tiled=True)
 
@@ -363,6 +435,18 @@
     return tuple(unpack_heads(in_hbm(attended))) + tuple(unpack_heads(grads))
 
 
+def two_exchanges(queries, keys, values, out_grad, key_blocks, dilation):
+    layouts = tuple(Packed(0, 4, i) for i in range(4))
+    my_head = lax.axis_index("seq")
+    lists, store, residue, offsets = index_tables(
+        lax.dynamic_index_in_dim(key_blocks, my_head, 0, keepdims=False),
+        lax.dynamic_index_in_dim(dilation, my_head, 0, keepdims=False),
+    )
+    tables = (layouts[1].positions(lists), layouts[2].positions(lists), store, residue, offsets)
+    packed = exchange(pack_heads(queries, keys, values, out_grad)).reshape(-1, BLOCK, HEAD_DIM)
+    return tuple(unpack_heads(exchange(head_at_once(packed, layouts, tables))))
+
+
 ALL_AT_ONCE = functools.partial(
     one_head, ((0, 1, 2),), (Packed(0, 3, 0), Packed(0, 3, 1), Packed(0, 3, 2))
 )
@@ -373,7 +457,7 @@
 
 def local(*arguments):
     odd = lax.axis_index("batch") % 2
-    return lax.cond(odd == 0, ALL_AT_ONCE, VALUES_FIRST, *arguments)
+    return lax.cond(odd == 0, ALL_AT_ONCE, two_exchanges, *arguments)
 
 
 def solution(mesh):

time: 230 us -> 222 us (0.965)
  the two profiles are of different devices: /device:TPU:1 before, /device:TPU:2 now
where the time goes in v5:
time: 222 us; the launch traced here: 221 us
  waiting for transfers between devices  132 us (59%)
  Pallas kernels  38.8 us (17%)
  starting transfers between devices  33.5 us (15%)
  local copies, waits for them, and re-layouts  9.58 us (4%)
  other arithmetic  4.72 us (2%)
    all_to_all x4, waiting for transfers between devices, exchange(): lax.all_to_all(by_device, 'seq', split_axis=0, concat_axis=0, tiled=True)  132 us
    all_to_all x4, starting transfers between devices, exchange(): lax.all_to_all(by_device, 'seq', split_axis=0, concat_axis=0, tiled=True)  33.5 us
    pallas_call x1, Pallas kernels, head_backward(): pl.pallas_call(body, grid=(pairs // PAIRS_PER_STEP,), in_specs=[SCALARS,...  17.8 us
    pallas_call x1, Pallas kernels, head_forward(): pl.pallas_call(body, grid=(pairs // PAIRS_PER_STEP,), in_specs=[SCALARS,...  11.4 us
    pallas_call x2, Pallas kernels, pack_heads(): pl.pallas_call(body, grid=(width // HEAD_DIM // HEADS_PER_STEP,), in_spec...  5.39 us
  transfers between devices with their start and end apart: 4, of which 3 were waited for; matrix products, arithmetic and copies ran while one was open for 5% of the time, Pallas kernels for 15%

profile of v5, /device:TPU:2, one launch (start us, length us, event | category | flops | bytes accessed | tf_op | source)
XLA Modules:
  0.0 221.1 jit_solution(16252993517222314981)
XLA Ops:
  0.6 220.4 %conditional.1 = ((bf16[128,4096]{1,0:T(8,128)(2,1)}, bf16[128,4096]{1,0:T(8,128)(2,1)}, bf16[128,4096]{1,0:T(8,128)(2,1)}, bf16[128,4096]{1,0:T(8,128)(2,1)})) conditional(s32[]{:T(128)} %convert_element_type.3, (s32[32,64,12]{1,0,2:T(8,128)}, s32[32]{0:T(128)}, bf16[128,4096]{1,0:T(8,128)(2,1)}, bf16[128,4096]{1,0:T(8,128)(2,1)}, ...), branch_computations={%region_0.1_spmd, %region_1.2_spmd} | conditional | flops 44000133120 | bytes 66045244 | solution.py:460
  0.7 3.3 %pack_heads.5 = bf16[32,3,128,128]{3,2,1,0:T(8,128)(2,1)} custom-call(bf16[128,4096]{1,0:T(8,128)(2,1)} %get-tuple-element.37.refs_0_, bf16[128,4096]{1,0:T(8,128)(2,1)} %get-tuple-element.38.refs_1_, bf16[128,4096]{1,0:T(8,128)(2,1)} %get-tuple-element.39.refs_2_), custom_call_target="tpu_custom_call" | custom-call | tf_op jit(solution)/shard_map/cond/branch_1_fun/pack_heads/pallas_call | solution.py:375
  3.9 11.8 %all-to-all-start.2 = ((bf16[32,3,128,128]{3,2,1,0:T(8,128)(2,1)}), bf16[32,3,128,128]{3,2,1,0:T(8,128)(2,1)S(1)}, u32[]{:S(2)}, u32[]{:S(2)}) async-start(bf16[32,3,128,128]{3,2,1,0:T(8,128)(2,1)} %pack_heads.5), calls=%async_computation.2 | async-start | bytes 6291456 | tf_op jit(solution)/shard_map/cond/branch_1_fun/all_to_all | solution.py:359
  17.7 1.4 copy.35
  19.0 0.8 dynamic-slice_compare_fusion.1
  19.8 0.8 dynamic-slice_maximum_fusion.1
  20.6 1.4 fusion.17
  22.0 1.0 copy.32
  23.0 1.5 broadcast_in_dim.38
  24.5 0.9 reshape.394
  25.4 1.0 copy.33
  26.4 2.1 pack_heads.4
  29.0 1.4 compare_select_fusion.1
  30.4 60.3 %all-to-all-done.2 = bf16[32,3,128,128]{3,2,1,0:T(8,128)(2,1)S(1)} async-done(((bf16[32,3,128,128]{3,2,1,0:T(8,128)(2,1)}), bf16[32,3,128,128]{3,2,1,0:T(8,128)(2,1)S(1)}, u32[]{:S(2)}, u32[]{:S(2)}) %all-to-all-start.2) | async-done | bytes 3145760 | tf_op jit(solution)/shard_map/cond/branch_1_fun/all_to_all | solution.py:359
  90.7 6.0 %all-to-all-start.4 = ((bf16[32,1,128,128]{3,2,1,0:T(8,128)(2,1)}), bf16[32,1,128,128]{3,2,1,0:T(8,128)(2,1)}, u32[]{:S(2)}, u32[]{:S(2)}) async-start(bf16[32,1,128,128]{3,2,1,0:T(8,128)(2,1)} %pack_heads.4), calls=%async_computation.4 | async-start | bytes 2097152 | tf_op jit(solution)/shard_map/cond/branch_1_fun/all_to_all | solution.py:359
  97.4 11.4 %head_forward.1 = (bf16[32,768,128]{2,1,0:T(8,128)(2,1)}, bf16[32,128,128]{2,1,0:T(8,128)(2,1)}) custom-call(s32[64,12]{1,0:T(8,128)S(1)} %get-tuple-element.33.k_load_ref, s32[64,12]{1,0:T(8,128)S(1)} %copy-done.1, s32[32,16,128]{2,1,0:T(8,128)S(1)} %pad.6.residue_ref, s32[2,64,128]{2,1,0:T(8,128)S(1)} %pad_add_fusion.1.offsets_ref, ...), custom_call_target="tpu_custom_call" | custom-call | flops 20000000000 | bytes 10000000 | tf_op jit(solution)/shard_map/cond/branch_1_fun/head_forward/pallas_call | solution.py:196
  108.8 5.9 %all-to-all-done.4 = bf16[32,1,128,128]{3,2,1,0:T(8,128)(2,1)} async-done(((bf16[32,1,128,128]{3,2,1,0:T(8,128)(2,1)}), bf16[32,1,128,128]{3,2,1,0:T(8,128)(2,1)}, u32[]{:S(2)}, u32[]{:S(2)}) %all-to-all-start.4) | async-done | bytes 1048608 | tf_op jit(solution)/shard_map/cond/branch_1_fun/all_to_all | solution.py:359
  114.8 5.9 %all-to-all-start.3 = ((bf16[32,1,128,128]{3,2,1,0:T(8,128)(2,1)}), bf16[32,1,128,128]{3,2,1,0:T(8,128)(2,1)}, u32[]{:S(2)}, u32[]{:S(2)}) async-start(bf16[32,1,128,128]{3,2,1,0:T(8,128)(2,1)} %bitcast.64), calls=%async_computation.3 | async-start | bytes 2097152 | tf_op jit(solution)/shard_map/cond/branch_1_fun/all_to_all | solution.py:359
  121.4 17.8 %head_backward.1 = bf16[32,3,128,128]{3,2,1,0:T(8,128)(2,1)S(1)} custom-call(s32[64,12]{1,0:T(8,128)S(1)} %get-tuple-element.33.k_load_ref, s32[64,12]{1,0:T(8,128)S(1)} %copy-done.2, s32[64,12]{1,0:T(8,128)S(1)} %get-tuple-element.41.store_ref, bf16[32,768,128]{2,1,0:T(8,128)(2,1)} %get-tuple-element.42.weights_ref, bf16[32,128,128]{2,1,0:T(8,128)(2,1)} %bitcast.11.g_ref, ...), custom_call_target="tpu_custom_call" | custom-call | flops 24000000000 | bytes 16000000 | tf_op jit(solution)/shard_map/cond/branch_1_fun/head_backward/pallas_call | solution.py:264
  139.2 1.6 copy-done
  140.9 9.9 %all-to-all-start.5 = ((bf16[32,3,128,128]{3,2,1,0:T(8,128)(2,1)}), bf16[32,3,128,128]{3,2,1,0:T(8,128)(2,1)S(1)}, u32[]{:S(2)}, u32[]{:S(2)}) async-start(bf16[32,3,128,128]{3,2,1,0:T(8,128)(2,1)} %copy-done), calls=%async_computation.5 | async-start | bytes 6291456 | tf_op jit(solution)/shard_map/cond/branch_1_fun/all_to_all | solution.py:359
  150.7 2.2 unpack_heads.4
  152.9 66.1 %all-to-all-done.5.packed_ref = bf16[32,3,128,128]{3,2,1,0:T(8,128)(2,1)S(1)} async-done(((bf16[32,3,128,128]{3,2,1,0:T(8,128)(2,1)}), bf16[32,3,128,128]{3,2,1,0:T(8,128)(2,1)S(1)}, u32[]{:S(2)}, u32[]{:S(2)}) %all-to-all-start.5) | async-done | bytes 3145760 | tf_op jit(solution)/shard_map/cond/branch_1_fun/all_to_all | solution.py:359
  219.0 2.1 unpack_heads.5
  (18 shorter events, 2.5 us)
Async XLA Ops:
  3.9 11.8 %copy-start.6 = (s32[32]{0:T(128)S(1)}, s32[32]{0:T(128)}, u32[]{:S(2)}) copy-start(s32[32]{0:T(128)} %get-tuple-element.32) | copy-start | bytes 388 | tf_op jit(solution)/shard_map/cond
  3.9 13.7 %copy-start.4 = (s32[32,64,12]{1,0,2:T(8,128)S(1)}, s32[32,64,12]{1,0,2:T(8,128)}, u32[]{:S(2)}) copy-start(s32[32,64,12]{1,0,2:T(8,128)} %get-tuple-element.90) | copy-start | bytes 294916 | tf_op jit(solution)/shard_map/cond
  3.9 86.7 %all-to-all-start.2 = ((bf16[32,3,128,128]{3,2,1,0:T(8,128)(2,1)}), bf16[32,3,128,128]{3,2,1,0:T(8,128)(2,1)S(1)}, u32[]{:S(2)}, u32[]{:S(2)}) async-start(bf16[32,3,128,128]{3,2,1,0:T(8,128)(2,1)} %pack_heads.5), calls=%async_computation.2 | async-start | bytes 6291456 | tf_op jit(solution)/shard_map/cond/branch_1_fun/all_to_all | solution.py:359
  90.7 24.1 %all-to-all-start.4 = ((bf16[32,1,128,128]{3,2,1,0:T(8,128)(2,1)}), bf16[32,1,128,128]{3,2,1,0:T(8,128)(2,1)}, u32[]{:S(2)}, u32[]{:S(2)}) async-start(bf16[32,1,128,128]{3,2,1,0:T(8,128)(2,1)} %pack_heads.4), calls=%async_computation.4 | async-start | bytes 2097152 | tf_op jit(solution)/shard_map/cond/branch_1_fun/all_to_all | solution.py:359
  96.7 0.8 copy-start.1
  114.8 26.1 %all-to-all-start.3 = ((bf16[32,1,128,128]{3,2,1,0:T(8,128)(2,1)}), bf16[32,1,128,128]{3,2,1,0:T(8,128)(2,1)}, u32[]{:S(2)}, u32[]{:S(2)}) async-start(bf16[32,1,128,128]{3,2,1,0:T(8,128)(2,1)} %bitcast.64), calls=%async_computation.3 | async-start | bytes 2097152 | tf_op jit(solution)/shard_map/cond/branch_1_fun/all_to_all | solution.py:359
  120.7 0.8 copy-start.2
  139.2 1.6 copy-start
  140.9 78.1 %all-to-all-start.5 = ((bf16[32,3,128,128]{3,2,1,0:T(8,128)(2,1)}), bf16[32,3,128,128]{3,2,1,0:T(8,128)(2,1)S(1)}, u32[]{:S(2)}, u32[]{:S(2)}) async-start(bf16[32,3,128,128]{3,2,1,0:T(8,128)(2,1)} %copy-done), calls=%async_computation.5 | async-start | bytes 6291456 | tf_op jit(solution)/shard_map/cond/branch_1_fun/all_to_all | solution.py:359

commit v6 on v5

--- a/solution.py
+++ b/solution.py
@@ -214,15 +214,42 @@
     )(k_load, v_load, residue, offsets, *packed)
 
 
+def send_step(stage_ref, out_ref, sems, pairs, arrays):
+    step = pl.program_id(0)
+    part = (pl.ds(step * pairs, pairs), pl.ds(0, arrays))
+    pltpu.make_async_copy(stage_ref.at[part], out_ref.at[part], sems.at[step]).start()
+
+
+def send_sums(stage_ref, out_ref, sems, steps, pairs, arrays, k_sum, v_sum):
+    copies = []
+    for step in range(steps):
+        part = (pl.ds(step * pairs, pairs), pl.ds(0, arrays))
+        copies.append(pltpu.make_async_copy(stage_ref.at[part], out_ref.at[part], sems.at[step]))
+    for step in range(steps):
+        rows = pl.ds(step * pairs, pairs)
+        blocks = pl.ds(2 * step * pairs, 2 * pairs)
+        by_pair = (pairs, PAIR, HEAD_DIM)
+        stage_ref[rows, arrays] = (k_sum[blocks] * SCALE).astype(bf16).reshape(by_pair)
+        stage_ref[rows, arrays + 1] = v_sum[blocks].astype(bf16).reshape(by_pair)
+        part = (rows, pl.ds(arrays, 2))
+        copy = pltpu.make_async_copy(stage_ref.at[part], out_ref.at[part], sems.at[steps + step])
+        copy.start()
+        copies.append(copy)
+    for copy in copies:
+        copy.wait()
+
+
 def head_backward(packed, layouts, g, o, weights, tables):
     k_load, v_load, store, _, _ = tables
     q_at, k_at, v_at = layouts
     pairs = g.shape[0]
     blocks = 2 * pairs
     grads_shape = (pairs, 3, PAIR, HEAD_DIM)
+    steps = pairs // PAIRS_PER_STEP
 
     def body(k_load_ref, v_load_ref, store_ref, weights_ref, g_ref, o_ref, *refs):
-        packed_refs, (grads_ref, k_sum, v_sum) = refs[: len(packed)], refs[len(packed) :]
+        packed_refs = refs[: len(packed)]
+        out_ref, k_sum, v_sum, grads_ref, sems = refs[len(packed) :]
         k_ref, v_ref = packed_refs[k_at.source], packed_refs[v_at.source]
 
         @pl.when(pl.program_id(0) == 0)
@@ -254,12 +281,11 @@
             grads_ref[first + u, 0] = (out * SCALE).astype(bf16)
 
         staggered(PAIRS_PER_STEP, (dweights, dscores, dqk))
-
-        @pl.when(pl.program_id(0) == pl.num_programs(0) - 1)
+        send_step(grads_ref, out_ref, sems, PAIRS_PER_STEP, 1)
+
+        @pl.when(pl.program_id(0) == steps - 1)
         def _():
-            by_pair = (pairs, PAIR, HEAD_DIM)
-            grads_ref[:, 1] = (k_sum[:blocks] * SCALE).astype(bf16).reshape(by_pair)
-            grads_ref[:, 2] = v_sum[:blocks].astype(bf16).reshape(by_pair)
+            send_sums(grads_ref, out_ref, sems, steps, PAIRS_PER_STEP, 1, k_sum, v_sum)
 
     return pl.pallas_call(
         body,
@@ -273,9 +299,10 @@
             per_step(o.shape),
         ]
         + [IN_VMEM] * len(packed),
-        out_specs=resident(grads_shape),
-        out_shape=jax.ShapeDtypeStruct(grads_shape, bf16),
-        scratch_shapes=[pltpu.VMEM((blocks + 1, BLOCK, HEAD_DIM), f32)] * 2,
+        out_specs=pl.BlockSpec(memory_space=pltpu.HBM),
+        out_shape=pltpu.HBM(grads_shape, bf16),
+        scratch_shapes=[pltpu.VMEM((blocks + 1, BLOCK, HEAD_DIM), f32)] * 2
+        + [pltpu.VMEM(grads_shape, bf16), pltpu.SemaphoreType.DMA((2 * steps,))],
         cost_estimate=pl.CostEstimate(
             flops=24_000_000_000, transcendentals=0, bytes_accessed=16_000_000
         ),
@@ -290,9 +317,11 @@
     pairs = residue.shape[0]
     blocks = 2 * pairs
     out_shape = (pairs, 4, PAIR, HEAD_DIM)
+    steps = pairs // PAIRS_AT_ONCE
 
     def body(
-        k_load_ref, v_load_ref, store_ref, residue_ref, offsets_ref, packed_ref, out_ref, k_sum, v_sum
+        k_load_ref, v_load_ref, store_ref, residue_ref, offsets_ref, packed_ref, sent_ref,
+        k_sum, v_sum, out_ref, sems,
     ):
         @pl.when(pl.program_id(0) == 0)
         def _():
@@ -333,20 +362,20 @@
             out_ref[first + u, 1] = (out * SCALE).astype(bf16)
 
         staggered(PAIRS_AT_ONCE, (scores, softmax, attend, dvalues, dqk))
-
-        @pl.when(pl.program_id(0) == pl.num_programs(0) - 1)
+        send_step(out_ref, sent_ref, sems, PAIRS_AT_ONCE, 2)
+
+        @pl.when(pl.program_id(0) == steps - 1)
         def _():
-            by_pair = (pairs, PAIR, HEAD_DIM)
-            out_ref[:, 2] = (k_sum[:blocks] * SCALE).astype(bf16).reshape(by_pair)
-            out_ref[:, 3] = v_sum[:blocks].astype(bf16).reshape(by_pair)
+            send_sums(out_ref, sent_ref, sems, steps, PAIRS_AT_ONCE, 2, k_sum, v_sum)
 
     return pl.pallas_call(
         body,
         grid=(pairs // PAIRS_AT_ONCE,),
         in_specs=[SCALARS] * 3 + [resident(residue.shape), resident(offsets.shape), IN_VMEM],
-        out_specs=resident(out_shape),
-        out_shape=jax.ShapeDtypeStruct(out_shape, bf16),
-        scratch_shapes=[pltpu.VMEM((blocks + 1, BLOCK, HEAD_DIM), f32)] * 2,
+        out_specs=pl.BlockSpec(memory_space=pltpu.HBM),
+        out_shape=pltpu.HBM(out_shape, bf16),
+        scratch_shapes=[pltpu.VMEM((blocks + 1, BLOCK, HEAD_DIM), f32)] * 2
+        + [pltpu.VMEM(out_shape, bf16), pltpu.SemaphoreType.DMA((2 * steps,))],
         cost_estimate=pl.CostEstimate(
             flops=44_000_000_000, transcendentals=3_000_000, bytes_accessed=10_000_000
         ),
@@ -427,6 +456,7 @@
         lax.dynamic_index_in_dim(dilation, my_head, 0, keepdims=False),
     )
     tables = (layouts[1].positions(lists), layouts[2].positions(lists), store, residue, offsets)
+    tables = tuple(in_hbm(x) for x in tables)
     packed_grad, tables = lax.optimization_barrier((pack_heads(out_grad), tables))
     g = exchange(packed_grad).reshape(-1, PAIR, HEAD_DIM)
     weights, o = head_forward(packed, layouts, tables)

time: 222 us -> 223 us (level)
  local copies, waits for them, and re-layouts: 9.58 us -> 7.15 us
    cond x10 -> x4, local copies, waits for them, and re-layouts: 3.14 us -> 0.01 us
  transfers between devices with their start and end apart: 4 -> 4, of which waited for: 3 -> 3; matrix products, arithmetic and copies ran while one was open for 5% -> 6% of each run, Pallas kernels for 15% -> 16%
where the time goes in v6:
time: 223 us; the launch traced here: 222 us
  waiting for transfers between devices  133 us (60%)
  Pallas kernels  40.7 us (18%)
  starting transfers between devices  33.4 us (15%)
  local copies, waits for them, and re-layouts  7.15 us (3%)
  other arithmetic  5.36 us (2%)
    all_to_all x4, waiting for transfers between devices, exchange(): lax.all_to_all(by_device, 'seq', split_axis=0, concat_axis=0, tiled=True)  133 us
    all_to_all x4, starting transfers between devices, exchange(): lax.all_to_all(by_device, 'seq', split_axis=0, concat_axis=0, tiled=True)  33.4 us
    pallas_call x1, Pallas kernels, head_backward(): pl.pallas_call(body, grid=(pairs // PAIRS_PER_STEP,), in_specs=[SCALARS,...  19.5 us
    pallas_call x1, Pallas kernels, head_forward(): pl.pallas_call(body, grid=(pairs // PAIRS_PER_STEP,), in_specs=[SCALARS,...  11.6 us
    pallas_call x2, Pallas kernels, pack_heads(): pl.pallas_call(body, grid=(width // HEAD_DIM // HEADS_PER_STEP,), in_spec...  5.39 us
  transfers between devices with their start and end apart: 4, of which 3 were waited for; matrix products, arithmetic and copies ran while one was open for 6% of the time, Pallas kernels for 16%

profile of v6, /device:TPU:2, one launch (start us, length us, event | category | flops | bytes accessed | tf_op | source)
XLA Modules:
  0.0 221.7 jit_solution(3928800250883981859)
XLA Ops:
  0.6 221.0 %conditional.1 = ((bf16[128,4096]{1,0:T(8,128)(2,1)}, bf16[128,4096]{1,0:T(8,128)(2,1)}, bf16[128,4096]{1,0:T(8,128)(2,1)}, bf16[128,4096]{1,0:T(8,128)(2,1)})) conditional(s32[]{:T(128)} %convert_element_type.3, (s32[32,64,12]{1,0,2:T(8,128)}, s32[32]{0:T(128)}, bf16[128,4096]{1,0:T(8,128)(2,1)}, bf16[128,4096]{1,0:T(8,128)(2,1)}, ...), branch_computations={%region_0.1_spmd, %region_1.2_spmd} | conditional | flops 44000133120 | bytes 53437672 | solution.py:490
  0.7 3.3 %pack_heads.5 = bf16[32,3,128,128]{3,2,1,0:T(8,128)(2,1)} custom-call(bf16[128,4096]{1,0:T(8,128)(2,1)} %get-tuple-element.37.refs_0_, bf16[128,4096]{1,0:T(8,128)(2,1)} %get-tuple-element.38.refs_1_, bf16[128,4096]{1,0:T(8,128)(2,1)} %get-tuple-element.39.refs_2_), custom_call_target="tpu_custom_call" | custom-call | tf_op jit(solution)/shard_map/cond/branch_1_fun/pack_heads/pallas_call | solution.py:404
  3.9 11.8 %all-to-all-start.2 = ((bf16[32,3,128,128]{3,2,1,0:T(8,128)(2,1)}), bf16[32,3,128,128]{3,2,1,0:T(8,128)(2,1)S(1)}, u32[]{:S(2)}, u32[]{:S(2)}) async-start(bf16[32,3,128,128]{3,2,1,0:T(8,128)(2,1)} %pack_heads.5), calls=%async_computation.2 | async-start | bytes 6291456 | tf_op jit(solution)/shard_map/cond/branch_1_fun/all_to_all | solution.py:388
  17.7 1.4 copy.35
  19.0 0.8 dynamic-slice_compare_fusion.1
  19.8 0.8 dynamic-slice_maximum_fusion.1
  20.6 1.4 fusion.17
  22.0 1.0 copy.32
  23.0 1.5 broadcast_in_dim.38
  24.5 0.9 reshape.394
  25.4 1.0 copy.33
  26.4 2.1 pack_heads.4
  28.6 0.7 pad.6.residue_ref
  30.3 1.4 compare_select_fusion.1
  31.7 59.0 %all-to-all-done.2 = bf16[32,3,128,128]{3,2,1,0:T(8,128)(2,1)S(1)} async-done(((bf16[32,3,128,128]{3,2,1,0:T(8,128)(2,1)}), bf16[32,3,128,128]{3,2,1,0:T(8,128)(2,1)S(1)}, u32[]{:S(2)}, u32[]{:S(2)}) %all-to-all-start.2) | async-done | bytes 3145760 | tf_op jit(solution)/shard_map/cond/branch_1_fun/all_to_all | solution.py:388
  90.7 6.0 %all-to-all-start.4 = ((bf16[32,1,128,128]{3,2,1,0:T(8,128)(2,1)}), bf16[32,1,128,128]{3,2,1,0:T(8,128)(2,1)}, u32[]{:S(2)}, u32[]{:S(2)}) async-start(bf16[32,1,128,128]{3,2,1,0:T(8,128)(2,1)} %pack_heads.4), calls=%async_computation.4 | async-start | bytes 2097152 | tf_op jit(solution)/shard_map/cond/branch_1_fun/all_to_all | solution.py:388
  96.7 11.6 %head_forward.1 = (bf16[32,768,128]{2,1,0:T(8,128)(2,1)}, bf16[32,128,128]{2,1,0:T(8,128)(2,1)}) custom-call(s32[64,12]{1,0:T(8,128)} %get-tuple-element.33.k_load_ref, s32[64,12]{1,0:T(8,128)} %get-tuple-element.34.v_load_ref, s32[32,16,128]{2,1,0:T(8,128)} %pad.6.residue_ref, s32[2,64,128]{2,1,0:T(8,128)} %pad_add_fusion.1.offsets_ref, ...), custom_call_target="tpu_custom_call" | custom-call | flops 20000000000 | bytes 10000000 | tf_op jit(solution)/shard_map/cond/branch_1_fun/head_forward/pallas_call | solution.py:196
  108.3 6.5 %all-to-all-done.4 = bf16[32,1,128,128]{3,2,1,0:T(8,128)(2,1)} async-done(((bf16[32,1,128,128]{3,2,1,0:T(8,128)(2,1)}), bf16[32,1,128,128]{3,2,1,0:T(8,128)(2,1)}, u32[]{:S(2)}, u32[]{:S(2)}) %all-to-all-start.4) | async-done | bytes 1048608 | tf_op jit(solution)/shard_map/cond/branch_1_fun/all_to_all | solution.py:388
  114.8 5.9 %all-to-all-start.3 = ((bf16[32,1,128,128]{3,2,1,0:T(8,128)(2,1)}), bf16[32,1,128,128]{3,2,1,0:T(8,128)(2,1)}, u32[]{:S(2)}, u32[]{:S(2)}) async-start(bf16[32,1,128,128]{3,2,1,0:T(8,128)(2,1)} %bitcast.64), calls=%async_computation.3 | async-start | bytes 2097152 | tf_op jit(solution)/shard_map/cond/branch_1_fun/all_to_all | solution.py:388
  120.7 19.5 %head_backward.1 = bf16[32,3,128,128]{3,2,1,0:T(8,128)(2,1)} custom-call(s32[64,12]{1,0:T(8,128)} %get-tuple-element.33.k_load_ref, s32[64,12]{1,0:T(8,128)} %get-tuple-element.34.v_load_ref, s32[64,12]{1,0:T(8,128)} %get-tuple-element.41.store_ref, bf16[32,768,128]{2,1,0:T(8,128)(2,1)} %get-tuple-element.42.weights_ref, ...), custom_call_target="tpu_custom_call" | custom-call | flops 24000000000 | bytes 16000000 | tf_op jit(solution)/shard_map/cond/branch_1_fun/head_backward/pallas_call | solution.py:290
  140.2 9.7 %all-to-all-start.5 = ((bf16[32,3,128,128]{3,2,1,0:T(8,128)(2,1)}), bf16[32,3,128,128]{3,2,1,0:T(8,128)(2,1)S(1)}, u32[]{:S(2)}, u32[]{:S(2)}) async-start(bf16[32,3,128,128]{3,2,1,0:T(8,128)(2,1)} %head_backward.1), calls=%async_computation.5 | async-start | bytes 6291456 | tf_op jit(solution)/shard_map/cond/branch_1_fun/all_to_all | solution.py:388
  149.9 2.2 unpack_heads.4
  152.1 67.5 %all-to-all-done.5.packed_ref = bf16[32,3,128,128]{3,2,1,0:T(8,128)(2,1)S(1)} async-done(((bf16[32,3,128,128]{3,2,1,0:T(8,128)(2,1)}), bf16[32,3,128,128]{3,2,1,0:T(8,128)(2,1)S(1)}, u32[]{:S(2)}, u32[]{:S(2)}) %all-to-all-start.5) | async-done | bytes 3145760 | tf_op jit(solution)/shard_map/cond/branch_1_fun/all_to_all | solution.py:388
  219.6 2.1 unpack_heads.5
  (12 shorter events, 1.6 us)
Async XLA Ops:
  3.9 11.8 %copy-start.3 = (s32[32]{0:T(128)S(1)}, s32[32]{0:T(128)}, u32[]{:S(2)}) copy-start(s32[32]{0:T(128)} %get-tuple-element.32) | copy-start | bytes 388 | tf_op jit(solution)/shard_map/cond
  3.9 13.7 %copy-start.1 = (s32[32,64,12]{1,0,2:T(8,128)S(1)}, s32[32,64,12]{1,0,2:T(8,128)}, u32[]{:S(2)}) copy-start(s32[32,64,12]{1,0,2:T(8,128)} %get-tuple-element.90) | copy-start | bytes 294916 | tf_op jit(solution)/shard_map/cond
  3.9 86.8 %all-to-all-start.2 = ((bf16[32,3,128,128]{3,2,1,0:T(8,128)(2,1)}), bf16[32,3,128,128]{3,2,1,0:T(8,128)(2,1)S(1)}, u32[]{:S(2)}, u32[]{:S(2)}) async-start(bf16[32,3,128,128]{3,2,1,0:T(8,128)(2,1)} %pack_heads.5), calls=%async_computation.2 | async-start | bytes 6291456 | tf_op jit(solution)/shard_map/cond/branch_1_fun/all_to_all | solution.py:388
  90.7 24.1 %all-to-all-start.4 = ((bf16[32,1,128,128]{3,2,1,0:T(8,128)(2,1)}), bf16[32,1,128,128]{3,2,1,0:T(8,128)(2,1)}, u32[]{:S(2)}, u32[]{:S(2)}) async-start(bf16[32,1,128,128]{3,2,1,0:T(8,128)(2,1)} %pack_heads.4), calls=%async_computation.4 | async-start | bytes 2097152 | tf_op jit(solution)/shard_map/cond/branch_1_fun/all_to_all | solution.py:388
  114.8 25.4 %all-to-all-start.3 = ((bf16[32,1,128,128]{3,2,1,0:T(8,128)(2,1)}), bf16[32,1,128,128]{3,2,1,0:T(8,128)(2,1)}, u32[]{:S(2)}, u32[]{:S(2)}) async-start(bf16[32,1,128,128]{3,2,1,0:T(8,128)(2,1)} %bitcast.64), calls=%async_computation.3 | async-start | bytes 2097152 | tf_op jit(solution)/shard_map/cond/branch_1_fun/all_to_all | solution.py:388
  140.2 79.4 %all-to-all-start.5 = ((bf16[32,3,128,128]{3,2,1,0:T(8,128)(2,1)}), bf16[32,3,128,128]{3,2,1,0:T(8,128)(2,1)S(1)}, u32[]{:S(2)}, u32[]{:S(2)}) async-start(bf16[32,3,128,128]{3,2,1,0:T(8,128)(2,1)} %head_backward.1), calls=%async_computation.5 | async-start | bytes 6291456 | tf_op jit(solution)/shard_map/cond/branch_1_fun/all_to_all | solution.py:388

commit v7 on v5

--- a/solution.py
+++ b/solution.py
@@ -302,21 +302,22 @@
         first = pl.program_id(0) * PAIRS_AT_ONCE
         held = {}
         weights = {}
+        products = {}
 
         def scores(u):
             q_rows = pair_queries(packed_ref, q_at, first + u)
             held[u] = pair_scores(k_load_ref, q_rows, packed_ref, first + u)
+            grads = pair_queries(packed_ref, g_at, first + u)
+            products[u] = pair_dweights(v_load_ref, packed_ref, grads, first + u)
 
         def softmax(u):
             weights[u] = pair_weights(residue_ref, offsets_ref, held[u], first + u)
-            grads = pair_queries(packed_ref, g_at, first + u)
-            held[u] = pair_dweights(v_load_ref, packed_ref, grads, first + u)
 
         def attend(u):
             out = rows_of_pair(weights[u], packed_ref, v_load_ref, first + u).astype(bf16)
             out_ref[first + u, 0] = out
             grads = pair_queries(packed_ref, g_at, first + u)
-            held[u] = pair_dscores(weights[u], held[u], grads, out)
+            held[u] = pair_dscores(weights[u], products.pop(u), grads, out)
 
         def dvalues(u):
             grads = pair_queries(packed_ref, g_at, first + u)
@@ -427,6 +428,7 @@
         lax.dynamic_index_in_dim(dilation, my_head, 0, keepdims=False),
     )
     tables = (layouts[1].positions(lists), layouts[2].positions(lists), store, residue, offsets)
+    tables = tuple(in_hbm(x) for x in tables)
     packed_grad, tables = lax.optimization_barrier((pack_heads(out_grad), tables))
     g = exchange(packed_grad).reshape(-1, PAIR, HEAD_DIM)
     weights, o = head_forward(packed, layouts, tables)

time: 222 us -> 221 us (level)
  transfers between devices with their start and end apart: 4 -> 4, of which waited for: 3 -> 3; matrix products, arithmetic and copies ran while one was open for 5% -> 6% of each run, Pallas kernels for 15% -> 16%
where the time goes in v7:
time: 221 us; the launch traced here: 219 us
  waiting for transfers between devices  131 us (59%)
  Pallas kernels  39.4 us (18%)
  starting transfers between devices  33.2 us (15%)
  local copies, waits for them, and re-layouts  8.77 us (4%)
  other arithmetic  5.35 us (2%)
    all_to_all x4, waiting for transfers between devices, exchange(): lax.all_to_all(by_device, 'seq', split_axis=0, concat_axis=0, tiled=True)  131 us
    all_to_all x4, starting transfers between devices, exchange(): lax.all_to_all(by_device, 'seq', split_axis=0, concat_axis=0, tiled=True)  33.2 us
    pallas_call x1, Pallas kernels, head_backward(): pl.pallas_call(body, grid=(pairs // PAIRS_PER_STEP,), in_specs=[SCALARS,...  18.2 us
    pallas_call x1, Pallas kernels, head_forward(): pl.pallas_call(body, grid=(pairs // PAIRS_PER_STEP,), in_specs=[SCALARS,...  11.6 us
    pallas_call x2, Pallas kernels, pack_heads(): pl.pallas_call(body, grid=(width // HEAD_DIM // HEADS_PER_STEP,), in_spec...  5.39 us
  transfers between devices with their start and end apart: 4, of which 3 were waited for; matrix products, arithmetic and copies ran while one was open for 6% of the time, Pallas kernels for 16%

profile of v7, /device:TPU:2, one launch (start us, length us, event | category | flops | bytes accessed | tf_op | source)
XLA Modules:
  0.0 219.4 jit_solution(1436902655831229102)
XLA Ops:
  0.6 218.8 %conditional.1 = ((bf16[128,4096]{1,0:T(8,128)(2,1)}, bf16[128,4096]{1,0:T(8,128)(2,1)}, bf16[128,4096]{1,0:T(8,128)(2,1)}, bf16[128,4096]{1,0:T(8,128)(2,1)})) conditional(s32[]{:T(128)} %convert_element_type.3, (s32[32,64,12]{1,0,2:T(8,128)}, s32[32]{0:T(128)}, bf16[128,4096]{1,0:T(8,128)(2,1)}, bf16[128,4096]{1,0:T(8,128)(2,1)}, ...), branch_computations={%region_0.1_spmd, %region_1.2_spmd} | conditional | flops 44000133120 | bytes 66020612 | solution.py:462
  0.7 3.3 %pack_heads.5 = bf16[32,3,128,128]{3,2,1,0:T(8,128)(2,1)} custom-call(bf16[128,4096]{1,0:T(8,128)(2,1)} %get-tuple-element.37.refs_0_, bf16[128,4096]{1,0:T(8,128)(2,1)} %get-tuple-element.38.refs_1_, bf16[128,4096]{1,0:T(8,128)(2,1)} %get-tuple-element.39.refs_2_), custom_call_target="tpu_custom_call" | custom-call | tf_op jit(solution)/shard_map/cond/branch_1_fun/pack_heads/pallas_call | solution.py:376
  3.9 11.8 %all-to-all-start.2 = ((bf16[32,3,128,128]{3,2,1,0:T(8,128)(2,1)}), bf16[32,3,128,128]{3,2,1,0:T(8,128)(2,1)S(1)}, u32[]{:S(2)}, u32[]{:S(2)}) async-start(bf16[32,3,128,128]{3,2,1,0:T(8,128)(2,1)} %pack_heads.5), calls=%async_computation.2 | async-start | bytes 6291456 | tf_op jit(solution)/shard_map/cond/branch_1_fun/all_to_all | solution.py:360
  17.7 1.4 copy.35
  19.0 0.8 dynamic-slice_compare_fusion.1
  19.8 0.8 dynamic-slice_maximum_fusion.1
  20.6 1.4 fusion.17
  22.0 1.0 copy.32
  23.0 1.5 broadcast_in_dim.38
  24.5 0.9 reshape.394
  25.4 1.0 copy.33
  26.4 2.1 pack_heads.4
  30.3 1.4 compare_select_fusion.1
  31.7 59.0 %all-to-all-done.2 = bf16[32,3,128,128]{3,2,1,0:T(8,128)(2,1)S(1)} async-done(((bf16[32,3,128,128]{3,2,1,0:T(8,128)(2,1)}), bf16[32,3,128,128]{3,2,1,0:T(8,128)(2,1)S(1)}, u32[]{:S(2)}, u32[]{:S(2)}) %all-to-all-start.2) | async-done | bytes 3145760 | tf_op jit(solution)/shard_map/cond/branch_1_fun/all_to_all | solution.py:360
  90.7 6.0 %all-to-all-start.4 = ((bf16[32,1,128,128]{3,2,1,0:T(8,128)(2,1)}), bf16[32,1,128,128]{3,2,1,0:T(8,128)(2,1)}, u32[]{:S(2)}, u32[]{:S(2)}) async-start(bf16[32,1,128,128]{3,2,1,0:T(8,128)(2,1)} %pack_heads.4), calls=%async_computation.4 | async-start | bytes 2097152 | tf_op jit(solution)/shard_map/cond/branch_1_fun/all_to_all | solution.py:360
  96.7 11.6 %head_forward.1 = (bf16[32,768,128]{2,1,0:T(8,128)(2,1)}, bf16[32,128,128]{2,1,0:T(8,128)(2,1)}) custom-call(s32[64,12]{1,0:T(8,128)} %get-tuple-element.33.k_load_ref, s32[64,12]{1,0:T(8,128)} %get-tuple-element.34.v_load_ref, s32[32,16,128]{2,1,0:T(8,128)} %pad.6.residue_ref, s32[2,64,128]{2,1,0:T(8,128)} %pad_add_fusion.1.offsets_ref, ...), custom_call_target="tpu_custom_call" | custom-call | flops 20000000000 | bytes 10000000 | tf_op jit(solution)/shard_map/cond/branch_1_fun/head_forward/pallas_call | solution.py:196
  108.2 6.5 %all-to-all-done.4 = bf16[32,1,128,128]{3,2,1,0:T(8,128)(2,1)} async-done(((bf16[32,1,128,128]{3,2,1,0:T(8,128)(2,1)}), bf16[32,1,128,128]{3,2,1,0:T(8,128)(2,1)}, u32[]{:S(2)}, u32[]{:S(2)}) %all-to-all-start.4) | async-done | bytes 1048608 | tf_op jit(solution)/shard_map/cond/branch_1_fun/all_to_all | solution.py:360
  114.8 5.9 %all-to-all-start.3 = ((bf16[32,1,128,128]{3,2,1,0:T(8,128)(2,1)}), bf16[32,1,128,128]{3,2,1,0:T(8,128)(2,1)}, u32[]{:S(2)}, u32[]{:S(2)}) async-start(bf16[32,1,128,128]{3,2,1,0:T(8,128)(2,1)} %bitcast.64), calls=%async_computation.3 | async-start | bytes 2097152 | tf_op jit(solution)/shard_map/cond/branch_1_fun/all_to_all | solution.py:360
  120.7 18.2 %head_backward.1 = bf16[32,3,128,128]{3,2,1,0:T(8,128)(2,1)S(1)} custom-call(s32[64,12]{1,0:T(8,128)} %get-tuple-element.33.k_load_ref, s32[64,12]{1,0:T(8,128)} %get-tuple-element.34.v_load_ref, s32[64,12]{1,0:T(8,128)} %get-tuple-element.41.store_ref, bf16[32,768,128]{2,1,0:T(8,128)(2,1)} %get-tuple-element.42.weights_ref, ...), custom_call_target="tpu_custom_call" | custom-call | flops 24000000000 | bytes 16000000 | tf_op jit(solution)/shard_map/cond/branch_1_fun/head_backward/pallas_call | solution.py:264
  138.9 1.6 copy-done
  140.6 9.5 %all-to-all-start.5 = ((bf16[32,3,128,128]{3,2,1,0:T(8,128)(2,1)}), bf16[32,3,128,128]{3,2,1,0:T(8,128)(2,1)S(1)}, u32[]{:S(2)}, u32[]{:S(2)}) async-start(bf16[32,3,128,128]{3,2,1,0:T(8,128)(2,1)} %copy-done), calls=%async_computation.5 | async-start | bytes 6291456 | tf_op jit(solution)/shard_map/cond/branch_1_fun/all_to_all | solution.py:360
  150.1 2.2 unpack_heads.4
  152.3 65.1 %all-to-all-done.5.packed_ref = bf16[32,3,128,128]{3,2,1,0:T(8,128)(2,1)S(1)} async-done(((bf16[32,3,128,128]{3,2,1,0:T(8,128)(2,1)}), bf16[32,3,128,128]{3,2,1,0:T(8,128)(2,1)S(1)}, u32[]{:S(2)}, u32[]{:S(2)}) %all-to-all-start.5) | async-done | bytes 3145760 | tf_op jit(solution)/shard_map/cond/branch_1_fun/all_to_all | solution.py:360
  217.4 2.1 unpack_heads.5
  (14 shorter events, 2.4 us)
Async XLA Ops:
  3.9 11.8 %copy-start.4 = (s32[32]{0:T(128)S(1)}, s32[32]{0:T(128)}, u32[]{:S(2)}) copy-start(s32[32]{0:T(128)} %get-tuple-element.32) | copy-start | bytes 388 | tf_op jit(solution)/shard_map/cond
  3.9 13.7 %copy-start.2 = (s32[32,64,12]{1,0,2:T(8,128)S(1)}, s32[32,64,12]{1,0,2:T(8,128)}, u32[]{:S(2)}) copy-start(s32[32,64,12]{1,0,2:T(8,128)} %get-tuple-element.90) | copy-start | bytes 294916 | tf_op jit(solution)/shard_map/cond
  3.9 86.8 %all-to-all-start.2 = ((bf16[32,3,128,128]{3,2,1,0:T(8,128)(2,1)}), bf16[32,3,128,128]{3,2,1,0:T(8,128)(2,1)S(1)}, u32[]{:S(2)}, u32[]{:S(2)}) async-start(bf16[32,3,128,128]{3,2,1,0:T(8,128)(2,1)} %pack_heads.5), calls=%async_computation.2 | async-start | bytes 6291456 | tf_op jit(solution)/shard_map/cond/branch_1_fun/all_to_all | solution.py:360
  90.7 24.1 %all-to-all-start.4 = ((bf16[32,1,128,128]{3,2,1,0:T(8,128)(2,1)}), bf16[32,1,128,128]{3,2,1,0:T(8,128)(2,1)}, u32[]{:S(2)}, u32[]{:S(2)}) async-start(bf16[32,1,128,128]{3,2,1,0:T(8,128)(2,1)} %pack_heads.4), calls=%async_computation.4 | async-start | bytes 2097152 | tf_op jit(solution)/shard_map/cond/branch_1_fun/all_to_all | solution.py:360
  114.8 25.8 %all-to-all-start.3 = ((bf16[32,1,128,128]{3,2,1,0:T(8,128)(2,1)}), bf16[32,1,128,128]{3,2,1,0:T(8,128)(2,1)}, u32[]{:S(2)}, u32[]{:S(2)}) async-start(bf16[32,1,128,128]{3,2,1,0:T(8,128)(2,1)} %bitcast.64), calls=%async_computation.3 | async-start | bytes 2097152 | tf_op jit(solution)/shard_map/cond/branch_1_fun/all_to_all | solution.py:360
  138.9 1.6 copy-start
  140.6 76.8 %all-to-all-start.5 = ((bf16[32,3,128,128]{3,2,1,0:T(8,128)(2,1)}), bf16[32,3,128,128]{3,2,1,0:T(8,128)(2,1)S(1)}, u32[]{:S(2)}, u32[]{:S(2)}) async-start(bf16[32,3,128,128]{3,2,1,0:T(8,128)(2,1)} %copy-done), calls=%async_computation.5 | async-start | bytes 6291456 | tf_op jit(solution)/shard_map/cond/branch_1_fun/all_to_all | solution.py:360
